TPU v7x, 512 devices: a whole 4x4x16 slice. The times are simulated.
512 devices in a mesh: expert: 128 (over x, z_lo, y), dp: 4 (over z_hi, core).
Axes of the slice: x: 4, y: 4, z: 16 (z_hi: 2, z_lo: 8; z = z_hi * 8 + z_lo), core: 2. Of those that a mesh axis runs over, the one named last changes fastest.
Arguments:
- tokens: bfloat16 [8192, 2048], P(('expert', 'dp')), may hold values from -6 to 6
- cotangent: bfloat16 [8192, 2048], P(('expert', 'dp')), may hold values from -6 to 6
- route_ids: int32 [8192, 8], P(('expert', 'dp')), may hold values from 0 to 127, all different within a row; in each aligned block of 16 rows (0 to 15, 16 to 31, ...) at most 2 rows name the same one
- route_gates: bfloat16 [8192, 8], P(('expert', 'dp')), may hold values from 0.019897461 to 0.5
- gate_up: bfloat16 [128, 2048, 1536], P('expert', 'dp'), may hold values from -0.125 to 0.125
- down: bfloat16 [128, 2048, 768], P('expert', 'dp'), may hold values from -6 to 6
- moment1: bfloat16 [128, 2048, 768], P('expert', 'dp'), may hold values from -4 to 4
- moment2: bfloat16 [128, 2048, 768], P('expert', 'dp'), may hold values from 0.049804688 to 0.5
- placement: int32 [128], replicated, may hold values from 0 to 127, each once
Outputs:
- rollout_down: bfloat16 [128, 2048, 768], P('expert', None, 'dp')
Inputs may be any that keep to these rules, and one draw needn't show every extreme that they name: `route_ids`: each row names 8 different experts; within the rows of one device no expert is named more than 2 times, a bound that some block reaches. `placement`: each expert exactly once.
All inputs are finite; a program needn't handle non-finite values.
Results may differ from a plain program's by a relative error of at most 0.003.
Values may be sent and summed in bfloat16 or wider, within the bound.
A program may use at most 64 MiB of HBM per device.

v0:
```python
import jax
import jax.numpy as jnp
from jax import lax
from jax.sharding import PartitionSpec as P

OPT_STEP = 2


BETA_ONE = 0.9
BETA_TWO = 0.95
ADAM_EPS = 1e-08
LEARN_RATE = 0.25


def shards(tokens, cotangent, route_ids, route_gates, gate_up, down, moment1, moment2, placement):
    experts = lax.axis_size("expert")
    tok_rows = tokens.shape[0]
    width = tokens.shape[1]
    top_count = route_ids.shape[1]
    hidden_units = down.shape[2]
    capacity = min(tok_rows, 2 * tok_rows * top_count // experts)
    total_slots = experts * capacity
    route_hits = jnp.sum(
        (route_ids[:, :, None] == jnp.arange(experts, dtype=jnp.int32)).astype(jnp.int32), axis=1
    )
    earlier_hits = jnp.cumsum(route_hits, axis=0) - route_hits
    slot_index = jnp.take_along_axis(earlier_hits, route_ids, axis=1)
    target_slot = route_ids * capacity + slot_index
    matched = (target_slot[:, :, None] == jnp.arange(total_slots, dtype=jnp.int32)).astype(
        jnp.float32
    )
    picker = jnp.sum(matched, axis=1).astype(jnp.bfloat16)
    contract_rows = (((0,), (0,)), ((), ()))
    send_rows = lax.dot_general(picker, tokens, contract_rows, preferred_element_type=jnp.float32)
    send_rows = send_rows.astype(jnp.bfloat16).reshape(experts, capacity, width)
    send_grads = lax.dot_general(
        picker, cotangent, contract_rows, preferred_element_type=jnp.float32
    )
    send_grads = send_grads.astype(jnp.bfloat16).reshape(experts, capacity, width)
    send_gates = jnp.sum(matched * route_gates.astype(jnp.float32)[:, :, None], axis=(0, 1))
    send_gates = send_gates.astype(jnp.bfloat16).reshape(experts, capacity)
    rows_in, grads_in, gates_in = (
        lax.all_to_all(send_rows, "expert", split_axis=0, concat_axis=0, tiled=True),
        lax.all_to_all(send_grads, "expert", split_axis=0, concat_axis=0, tiled=True),
        lax.all_to_all(send_gates, "expert", split_axis=0, concat_axis=0, tiled=True),
    )
    rows_flat = rows_in.reshape(total_slots, width)
    pre_all = jnp.dot(
        rows_flat,
        lax.all_gather(gate_up, "dp", axis=1, tiled=True)[0],
        preferred_element_type=jnp.float32,
    )
    hidden = (jax.nn.silu(pre_all[:, :hidden_units]) * pre_all[:, hidden_units:]).astype(
        jnp.bfloat16
    )
    scaled = gates_in.reshape(total_slots, 1).astype(jnp.float32) * grads_in.reshape(
        total_slots, width
    ).astype(jnp.float32)
    scaled = scaled.astype(jnp.bfloat16)
    grad_share = lax.psum_scatter(
        lax.dot_general(scaled, hidden, contract_rows, preferred_element_type=jnp.float32).astype(
            jnp.bfloat16
        ),
        "dp",
        scatter_dimension=0,
        tiled=True,
    ).astype(jnp.float32)
    correct_one = 1.0 - BETA_ONE**OPT_STEP
    correct_two = 1.0 - BETA_TWO**OPT_STEP
    first = BETA_ONE * moment1[0].astype(jnp.float32) + (1.0 - BETA_ONE) * grad_share
    second = BETA_TWO * moment2[0].astype(jnp.float32) + (1.0 - BETA_TWO) * grad_share * grad_share
    direction = first / correct_one / (jnp.sqrt(second / correct_two) + ADAM_EPS)
    updated = (down[0].astype(jnp.float32) - LEARN_RATE * direction).astype(jnp.bfloat16)
    column_block = lax.all_to_all(updated, "dp", split_axis=1, concat_axis=0, tiled=True)
    block_cols = column_block.shape[1]
    piece_flat = column_block.reshape(experts, width * block_cols // experts)
    spread = lax.all_to_all(piece_flat, "expert", split_axis=0, concat_axis=0, tiled=True)
    picked = jnp.take(spread, placement, axis=0)
    landed = lax.all_to_all(picked, "expert", split_axis=0, concat_axis=0, tiled=True)
    return landed.reshape(1, width, block_cols)


def solution(mesh):
    placed = (
        P(("expert", "dp"), None),
        P(("expert", "dp"), None),
        P(("expert", "dp"), None),
        P(("expert", "dp"), None),
        P("expert", "dp", None),
        P("expert", "dp", None),
        P("expert", "dp", None),
        P("expert", "dp", None),
        P(),
    )
    return jax.shard_map(
        shards, mesh=mesh, in_specs=placed, out_specs=P("expert", None, "dp"), check_vma=False
    )
```

profile of v0, /device:TPU:1, one launch (start us, length us, event | category | flops | bytes accessed | tf_op | source)
XLA Modules:
  0.0 586.9 jit_solution(1576552684572793220)
XLA Ops:
  6.5 0.7 all-gather.2.cloned.1.call-update
  7.3 0.1 convert_reduce_fusion.2
  7.6 0.1 reshape.117
  7.7 1.2 gather_fusion.1
  8.9 0.1 reshape.120
  9.1 0.1 copy.50
  9.2 0.1 copy.51
  9.2 0.1 select_reduce_fusion
  9.4 0.8 convert_element_type.102
  10.2 20.4 %all-to-all-start = ((bf16[128,1,2]{2,1,0:T(2,128)(2,1)}), bf16[128,1,2]{2,1,0:T(2,128)(2,1)S(1)}, u32[]{:S(2)}, u32[]{:S(2)}) async-start(bf16[128,1,2]{2,1,0:T(2,128)(2,1)} %convert_element_type.102), calls=%async_computation | async-start | bytes 131072 | tf_op jit(solution)/shard_map/all_to_all | solution.py:45
  30.6 0.5 convolution_convert_fusion.1
  31.1 1.5 reshape.103
  32.6 11.4 %all-to-all-done = bf16[128,1,2]{2,1,0:T(2,128)(2,1)S(1)} async-done(((bf16[128,1,2]{2,1,0:T(2,128)(2,1)}), bf16[128,1,2]{2,1,0:T(2,128)(2,1)S(1)}, u32[]{:S(2)}, u32[]{:S(2)}) %all-to-all-start) | async-done | bytes 544 | tf_op jit(solution)/shard_map/all_to_all | solution.py:45
  44.0 6.2 %all-to-all-start.2 = ((bf16[128,2,2048]{2,1,0:T(2,128)(2,1)}), bf16[128,2,2048]{2,1,0:T(2,128)(2,1)S(1)}, u32[]{:S(2)}, u32[]{:S(2)}) async-start(bf16[128,2,2048]{2,1,0:T(2,128)(2,1)} %reshape.103), calls=%async_computation.2 | async-start | bytes 2097152 | tf_op jit(solution)/shard_map/all_to_all | solution.py:43
  50.2 0.5 convolution_convert_fusion.2
  50.6 1.5 reshape.102
  52.1 171.0 %all-to-all-done.2 = bf16[128,2,2048]{2,1,0:T(2,128)(2,1)S(1)} async-done(((bf16[128,2,2048]{2,1,0:T(2,128)(2,1)}), bf16[128,2,2048]{2,1,0:T(2,128)(2,1)S(1)}, u32[]{:S(2)}, u32[]{:S(2)}) %all-to-all-start.2) | async-done | bytes 1048608 | tf_op jit(solution)/shard_map/all_to_all | solution.py:43
  223.2 8.1 %all-to-all-start.1 = ((bf16[128,2,2048]{2,1,0:T(2,128)(2,1)}), bf16[128,2,2048]{2,1,0:T(2,128)(2,1)S(1)}, u32[]{:S(2)}, u32[]{:S(2)}) async-start(bf16[128,2,2048]{2,1,0:T(2,128)(2,1)} %reshape.102), calls=%async_computation.1 | async-start | bytes 2097152 | tf_op jit(solution)/shard_map/all_to_all | solution.py:44
  231.2 0.2 reduce-scatter.2.cloned.1.call-start
  231.5 0.2 convert_reduce_fusion.1
  231.7 0.1 reshape.107
  231.8 1.2 reshape.104
  233.0 50.2 %all-to-all-done.1 = bf16[128,2,2048]{2,1,0:T(2,128)(2,1)S(1)} async-done(((bf16[128,2,2048]{2,1,0:T(2,128)(2,1)}), bf16[128,2,2048]{2,1,0:T(2,128)(2,1)S(1)}, u32[]{:S(2)}, u32[]{:S(2)}) %all-to-all-start.1) | async-done | bytes 1048608 | tf_op jit(solution)/shard_map/all_to_all | solution.py:44
  283.2 0.3 reshape.108
  283.5 4.9 fusion
  288.5 2.9 convolution_convert_fusion
  291.3 115.2 %reduce-scatter.2.cloned.1.call-done = bf16[512,768]{1,0:T(8,128)(2,1)} async-done(((bf16[2048,768]{1,0:T(8,128)(2,1)}), bf16[512,768]{1,0:T(8,128)(2,1)}) %reduce-scatter.2.cloned.1.call-update) | async-done | bytes 786448 | tf_op jit(solution)/shard_map/reduce_scatter | solution.py:60
  406.6 2.5 fusion.11
  409.1 0.3 copy.53
  409.3 42.3 %all_to_all.51 = bf16[512,4,192]{0,2,1:T(8,128)(2,1)S(1)} all-to-all(bf16[512,4,192]{0,2,1:T(8,128)(2,1)S(1)} %bitcast.32), channel_id=1, replica_groups=mesh['expert'=128,'dp'=4] {'dp'}, dimensions={1} | all-to-all | bytes 1572864 | tf_op jit(solution)/shard_map/all_to_all | solution.py:74
  451.6 0.5 copy.54
  452.2 1.4 all_to_all.44
  453.6 0.6 broadcast.72
  454.2 5.4 reduce.5
  459.6 1.4 reshape.137
  461.0 15.9 %all-to-all-start.4 = ((bf16[128,2,1536]{2,1,0:T(2,128)(2,1)}), bf16[128,2,1536]{2,1,0:T(2,128)(2,1)S(1)}, u32[]{:S(2)}, u32[]{:S(2)}) async-start(bf16[128,2,1536]{2,1,0:T(2,128)(2,1)} %reshape.137), calls=%async_computation.5 | async-start | bytes 1572864 | tf_op jit(solution)/shard_map/all_to_all | solution.py:77
  477.0 41.4 %all-to-all-done.4 = bf16[128,2,1536]{2,1,0:T(2,128)(2,1)S(1)} async-done(((bf16[128,2,1536]{2,1,0:T(2,128)(2,1)}), bf16[128,2,1536]{2,1,0:T(2,128)(2,1)S(1)}, u32[]{:S(2)}, u32[]{:S(2)}) %all-to-all-start.4) | async-done | bytes 786464 | tf_op jit(solution)/shard_map/all_to_all | solution.py:77
  518.4 0.6 reshape.138
  519.1 0.2 copy.60
  519.3 1.0 gather_fusion
  520.3 0.1 bitcast_select_fusion
  520.5 1.2 reduce.6
  521.7 0.6 reshape.139
  522.3 50.1 %all_to_all.52 = bf16[128,2,1536]{2,1,0:T(2,128)(2,1)S(1)} all-to-all(bf16[128,2,1536]{2,1,0:T(2,128)(2,1)S(1)} %reshape.139), channel_id=1, replica_groups=mesh['expert'=128,'dp'=4] {'expert'}, dimensions={0} | all-to-all | bytes 1572864 | tf_op jit(solution)/shard_map/all_to_all | solution.py:79
  572.4 0.6 reshape.140
  573.0 4.7 reduce.1
  577.7 1.1 reshape.105
  578.9 1.2 copy.57
  (29 shorter events, 0.4 us)
Async XLA Ops:
  6.5 24.1 %copy-start = (bf16[16,2048]{1,0:T(8,128)(2,1)S(1)}, bf16[16,2048]{1,0:T(8,128)(2,1)}, u32[]{:S(2)}) copy-start(bf16[16,2048]{1,0:T(8,128)(2,1)} %param.9) | copy-start | bytes 196612
  6.5 0.7 copy-start.5
  6.5 277.0 %all-gather.2.cloned.1.call-start = ((), (), s32[]{:S(2)}) async-start(), calls=%async_computation.7 | async-start | bytes 7864320 | tf_op jit(solution)/shard_map/all_gather | solution.py:50
  7.7 1.5 copy-start.6
  10.2 33.8 %all-to-all-start = ((bf16[128,1,2]{2,1,0:T(2,128)(2,1)}), bf16[128,1,2]{2,1,0:T(2,128)(2,1)S(1)}, u32[]{:S(2)}, u32[]{:S(2)}) async-start(bf16[128,1,2]{2,1,0:T(2,128)(2,1)} %convert_element_type.102), calls=%async_computation | async-start | bytes 131072 | tf_op jit(solution)/shard_map/all_to_all | solution.py:45
  31.1 19.1 %copy-start.4 = (bf16[16,2048]{1,0:T(8,128)(2,1)S(1)}, bf16[16,2048]{1,0:T(8,128)(2,1)}, u32[]{:S(2)}) copy-start(bf16[16,2048]{1,0:T(8,128)(2,1)} %param.10) | copy-start | bytes 196612
  44.0 179.2 %all-to-all-start.2 = ((bf16[128,2,2048]{2,1,0:T(2,128)(2,1)}), bf16[128,2,2048]{2,1,0:T(2,128)(2,1)S(1)}, u32[]{:S(2)}, u32[]{:S(2)}) async-start(bf16[128,2,2048]{2,1,0:T(2,128)(2,1)} %reshape.103), calls=%async_computation.2 | async-start | bytes 2097152 | tf_op jit(solution)/shard_map/all_to_all | solution.py:43
  223.2 60.0 %all-to-all-start.1 = ((bf16[128,2,2048]{2,1,0:T(2,128)(2,1)}), bf16[128,2,2048]{2,1,0:T(2,128)(2,1)S(1)}, u32[]{:S(2)}, u32[]{:S(2)}) async-start(bf16[128,2,2048]{2,1,0:T(2,128)(2,1)} %reshape.102), calls=%async_computation.1 | async-start | bytes 2097152 | tf_op jit(solution)/shard_map/all_to_all | solution.py:44
  231.2 175.3 %reduce-scatter.2.cloned.1.call-start = ((), (), s32[]{:S(2)}) async-start(), calls=%async_computation.8 | async-start | bytes 3932160 | tf_op jit(solution)/shard_map/reduce_scatter | solution.py:60
  291.3 115.2 %copy-start.1 = (bf16[1,512,768]{2,1,0:T(8,128)(2,1)S(1)}, bf16[1,512,768]{2,1,0:T(8,128)(2,1)}, u32[]{:S(2)}) copy-start(bf16[1,512,768]{2,1,0:T(8,128)(2,1)} %param.16) | copy-start | bytes 2359300
  291.3 115.2 %copy-start.2 = (bf16[1,512,768]{2,1,0:T(8,128)(2,1)S(1)}, bf16[1,512,768]{2,1,0:T(8,128)(2,1)}, u32[]{:S(2)}) copy-start(bf16[1,512,768]{2,1,0:T(8,128)(2,1)} %param.15) | copy-start | bytes 2359300
  291.3 115.2 %copy-start.3 = (bf16[1,512,768]{2,1,0:T(8,128)(2,1)S(1)}, bf16[1,512,768]{2,1,0:T(8,128)(2,1)}, u32[]{:S(2)}) copy-start(bf16[1,512,768]{2,1,0:T(8,128)(2,1)} %param.14) | copy-start | bytes 2359300
  459.6 17.4 %copy-start.7 = (s32[128]{0:T(128)S(1)}, s32[128]{0:T(128)}, u32[]{:S(2)}) copy-start(s32[128]{0:T(128)} %param.17) | copy-start | bytes 1540
  461.0 57.4 %all-to-all-start.4 = ((bf16[128,2,1536]{2,1,0:T(2,128)(2,1)}), bf16[128,2,1536]{2,1,0:T(2,128)(2,1)S(1)}, u32[]{:S(2)}, u32[]{:S(2)}) async-start(bf16[128,2,1536]{2,1,0:T(2,128)(2,1)} %reshape.137), calls=%async_computation.5 | async-start | bytes 1572864 | tf_op jit(solution)/shard_map/all_to_all | solution.py:77
Sparse Core Ops, SparseCore 0:
  9.4 141.1 all-gather.1
  291.5 115.0 reduce-scatter.1
where the time goes:
time: 587 us
  waiting for transfers between devices  390 us (66%)
  blocking collectives  92.4 us (16%)
  starting transfers between devices  50.8 us (9%)
  local copies, waits for them, and re-layouts  17.1 us (3%)
  other arithmetic  14.5 us (2%)
  between operations  13.7 us (2%)
  matrix products  8.67 us (1%)
    all_to_all x1, waiting for transfers between devices, shards(): lax.all_to_all(send_rows, 'expert', split_axis=0, concat_axis=0, tiled=True)  171 us
    reduce_scatter x1, waiting for transfers between devices, shards(): lax.psum_scatter(lax.dot_general(scaled, hidden, contract_rows, preferred...  115 us
    all_to_all x1, waiting for transfers between devices, shards(): lax.all_to_all(send_grads, 'expert', split_axis=0, concat_axis=0, tiled=T...  50.2 us
    all_to_all x1, blocking collectives, shards(): lax.all_to_all(picked, 'expert', split_axis=0, concat_axis=0, tiled=True)  50.1 us
    all_to_all x1, blocking collectives, shards(): lax.all_to_all(updated, 'dp', split_axis=1, concat_axis=0, tiled=True)  42.3 us
    all_to_all x1, waiting for transfers between devices, shards(): lax.all_to_all(piece_flat, 'expert', split_axis=0, concat_axis=0, tiled=T...  41.4 us
    all_to_all x1, starting transfers between devices, shards(): lax.all_to_all(send_gates, 'expert', split_axis=0, concat_axis=0, tiled=T...  20.4 us
    all_to_all x1, starting transfers between devices, shards(): lax.all_to_all(piece_flat, 'expert', split_axis=0, concat_axis=0, tiled=T...  15.9 us
  transfers between devices with their start and end apart: 6, of which 5 were waited for; matrix products, arithmetic and copies ran while one was open for 1% of the time, Pallas kernels for 0%

commit v1 on v0

v1 whole, which is shorter than its diff:
```python
import jax
import jax.numpy as jnp
from jax import lax
from jax.sharding import Mesh, PartitionSpec as P

OPT_STEP = 2


BETA_ONE = 0.9
BETA_TWO = 0.95
ADAM_EPS = 1e-08
LEARN_RATE = 0.25

DP = ("zh", "core")
PLANE = ("x", "y")
EXPERT = ("x", "zl", "y")
CAP = 2
META = 128

contract_rows = (((0,), (0,)), ((), ()))


def pickers(meta, blocks, block_rows, top):
    plane = lax.axis_size(PLANE)
    wide = meta.shape[0]
    ids = meta[:, :top].astype(jnp.int32)
    gates = meta[:, top : 2 * top].astype(jnp.float32)
    place = jnp.arange(plane, dtype=jnp.int32)
    y_size = lax.axis_size("y")
    wanted = (place // y_size * lax.axis_size("zl") + lax.axis_index("zl")) * y_size + place % y_size
    match = (ids[:, :, None] == wanted).astype(jnp.float32)
    hits = jnp.sum(match, axis=1)
    worth = jnp.sum(match * gates[:, :, None], axis=1)
    token = jnp.arange(wide, dtype=jnp.int32)
    own_block = token // block_rows
    before = ((own_block[:, None] == own_block[None, :]) & (token[None, :] < token[:, None])).astype(jnp.bfloat16)
    earlier = jnp.dot(before, hits.astype(jnp.bfloat16), preferred_element_type=jnp.float32)
    row = jnp.arange(plane * blocks * CAP, dtype=jnp.int32)
    row_place = row // (blocks * CAP)
    spread = (row_place[:, None] == place[None, :]).astype(jnp.bfloat16)
    take = lambda v: lax.dot_general(
        spread, v.astype(jnp.bfloat16), (((1,), (1,)), ((), ())), preferred_element_type=jnp.float32
    )
    here = (row // CAP % blocks)[:, None] == own_block[None, :]
    slot = jnp.where(hits > 0, earlier, -1.0)
    chosen = here & (take(slot) == (row % CAP)[:, None].astype(jnp.float32))
    one_hot = chosen.astype(jnp.bfloat16)
    return one_hot, jnp.where(chosen, take(worth), 0.0).astype(jnp.bfloat16)


def shards(tokens, cotangent, route_ids, route_gates, gate_up, down, moment1, moment2, placement):
    tok_rows, width = tokens.shape
    top = route_ids.shape[1]
    hidden_units = down.shape[2]
    groups = lax.axis_size(DP)
    line = lax.axis_size("zl")
    plane = lax.axis_size(PLANE)
    experts = lax.axis_size(EXPERT)
    share = width // groups
    bf16 = jnp.bfloat16

    meta = jnp.concatenate(
        [route_ids.astype(bf16), route_gates, jnp.zeros((tok_rows, META - 2 * top), bf16)], axis=1
    )
    tok_pack = lax.all_gather(jnp.concatenate([tokens, meta], axis=1), "zl", axis=0, tiled=True)

    cot_parts = cotangent.reshape(tok_rows, groups, share).transpose(1, 0, 2)
    cot_parts = jnp.concatenate(
        [cot_parts, jnp.broadcast_to(meta[None], (groups, tok_rows, META))], axis=2
    )
    cot_parts = lax.all_to_all(cot_parts, DP, split_axis=0, concat_axis=0, tiled=True)
    cot_pack = lax.all_gather(
        cot_parts.reshape(groups * tok_rows, share + META), "zl", axis=0, tiled=True
    )

    gate_up, cot_pack, tok_pack = lax.optimization_barrier((gate_up, cot_pack, tok_pack))
    weights = lax.all_gather(gate_up[0], DP, axis=0, tiled=True)

    tok_pick, _ = pickers(tok_pack[:, width:], line, tok_rows, top)
    rows = jnp.dot(tok_pick, tok_pack[:, :width], preferred_element_type=jnp.float32).astype(bf16)
    rows = lax.all_to_all(
        rows.reshape(plane, line * CAP, width), PLANE, split_axis=0, concat_axis=0, tiled=True
    ).reshape(plane * line * CAP, width)

    _, cot_pick = pickers(cot_pack[:, share:], line * groups, tok_rows, top)
    scaled = jnp.dot(cot_pick, cot_pack[:, :share], preferred_element_type=jnp.float32).astype(bf16)
    scaled = lax.all_to_all(
        scaled.reshape(plane, line * groups * CAP, share), PLANE, split_axis=0, concat_axis=0, tiled=True
    )
    scaled = scaled.reshape(plane * line, groups, CAP, share).transpose(1, 0, 2, 3)
    scaled = scaled.reshape(groups * plane * line * CAP, share)

    pre = jnp.dot(rows, weights, preferred_element_type=jnp.float32)
    hidden = (jax.nn.silu(pre[:, :hidden_units]) * pre[:, hidden_units:]).astype(bf16)
    hidden = lax.all_gather(hidden, DP, axis=0, tiled=True)
    grad = lax.dot_general(scaled, hidden, contract_rows, preferred_element_type=jnp.float32)

    correct_one = 1.0 - BETA_ONE**OPT_STEP
    correct_two = 1.0 - BETA_TWO**OPT_STEP
    first = BETA_ONE * moment1[0].astype(jnp.float32) + (1.0 - BETA_ONE) * grad
    second = BETA_TWO * moment2[0].astype(jnp.float32) + (1.0 - BETA_TWO) * grad * grad
    direction = first / correct_one / (jnp.sqrt(second / correct_two) + ADAM_EPS)
    updated = (down[0].astype(jnp.float32) - LEARN_RATE * direction).astype(bf16)

    block_cols = hidden_units // groups
    piece_rows = share // experts
    pieces = updated.reshape(experts, piece_rows, groups, block_cols).transpose(0, 2, 1, 3)
    pieces = pieces.reshape(experts * groups, piece_rows * block_cols)
    spread = lax.all_to_all(pieces, EXPERT + DP, split_axis=0, concat_axis=0, tiled=True)
    spread = spread.reshape(experts, groups * piece_rows * block_cols)
    picked = jnp.take(spread, placement, axis=0)
    landed = lax.all_to_all(picked, EXPERT, split_axis=0, concat_axis=0, tiled=True)
    landed = landed.reshape(experts, groups, piece_rows, block_cols).transpose(1, 0, 2, 3)
    return landed.reshape(1, width, block_cols)


def solution(mesh):
    grid = Mesh(mesh.devices.reshape(4, 8, 4, 2, 2), EXPERT + DP)
    every = P(EXPERT + DP, None)
    owned = P(EXPERT, DP, None)
    placed = (every, every, every, every, owned, owned, owned, owned, P())
    return jax.shard_map(
        shards, mesh=grid, in_specs=placed, out_specs=P(EXPERT, None, DP), check_vma=False
    )
```

time: 587 us -> 496 us (0.84)
  waiting for transfers between devices: 390 us -> 239 us
  blocking collectives: 92.4 us -> 172 us
  starting transfers between devices: 50.8 us -> 27.1 us
    all_to_all x4 -> x2, waiting for transfers between devices: 274 us -> 46.2 us  [the longest x1 46.2 us: shards(): lax.all_to_all(pieces, EXPERT + DP, split_axis=0, concat_axis=0, tiled=True)]
    all_gather x1 -> x2, waiting for transfers between devices: 0.02 us -> 193 us  [the longest x1 156 us: shards(): weights = lax.all_gather(gate_up[0], DP, axis=0, tiled=True)]
    reduce_scatter x1 -> x0, waiting for transfers between devices: 115 us -> none  [shards(): lax.psum_scatter(lax.dot_general(scaled, hidden, contract_rows, preferred...]
    all_gather x0 -> x2, blocking collectives: none -> 85.7 us  [the longest x1 43.4 us: shards(): lax.all_gather(cot_parts.reshape(groups * tok_rows, share + META), 'zl',...]
    all_to_all x4 -> x2, starting transfers between devices: 50.6 us -> 27 us  [the longest x1 16.6 us: shards(): lax.all_to_all(cot_parts, DP, split_axis=0, concat_axis=0, tiled=True)]
    all_to_all x2 -> x3, blocking collectives: 92.4 us -> 85.9 us  [the longest x1 48.3 us: shards(): lax.all_to_all(picked, EXPERT, split_axis=0, concat_axis=0, tiled=True)]
  transfers between devices with their start and end apart: 6 -> 4, of which waited for: 5 -> 3; matrix products, arithmetic and copies ran while one was open for 1% -> 1% of each run, Pallas kernels for 0% -> 0%
where the time goes in v1:
time: 496 us
  waiting for transfers between devices  239 us (48%)
  blocking collectives  172 us (35%)
  starting transfers between devices  27.1 us (5%)
  local copies, waits for them, and re-layouts  18.6 us (4%)
  between operations  13.7 us (3%)
  other arithmetic  13.2 us (3%)
  matrix products  12 us (2%)
    all_gather x1, waiting for transfers between devices, shards(): weights = lax.all_gather(gate_up[0], DP, axis=0, tiled=True)  156 us
    all_to_all x1, blocking collectives, shards(): lax.all_to_all(picked, EXPERT, split_axis=0, concat_axis=0, tiled=True)  48.3 us
    all_to_all x1, waiting for transfers between devices, shards(): lax.all_to_all(pieces, EXPERT + DP, split_axis=0, concat_axis=0, tiled=True)  46.2 us
    all_gather x1, blocking collectives, shards(): lax.all_gather(cot_parts.reshape(groups * tok_rows, share + META), 'zl',...  43.4 us
    all_gather x1, blocking collectives, shards(): lax.all_gather(jnp.concatenate([tokens, meta], axis=1), 'zl', axis=0, til...  42.3 us
    all_gather x1, waiting for transfers between devices, shards(): hidden = lax.all_gather(hidden, DP, axis=0, tiled=True)  37.2 us
    all_to_all x1, blocking collectives, shards(): lax.all_to_all(scaled.reshape(plane, line * groups * CAP, share), PLANE,...  19.4 us
    all_to_all x1, blocking collectives, shards(): lax.all_to_all(rows.reshape(plane, line * CAP, width), PLANE, split_axis=...  18.3 us
  transfers between devices with their start and end apart: 4, of which 3 were waited for; matrix products, arithmetic and copies ran while one was open for 1% of the time, Pallas kernels for 0%

profile of v1, /device:TPU:1, one launch (start us, length us, event | category | flops | bytes accessed | tf_op | source)
XLA Modules:
  0.0 495.7 jit_solution(6455398087655121743)
XLA Ops:
  6.5 0.8 copy.84
  7.3 0.8 copy.83
  8.1 0.9 reshape.250
  8.9 0.1 pad_maximum_fusion.1
  9.1 0.6 copy.85
  9.7 16.6 %all-to-all-start = ((bf16[4,16,640]{2,1,0:T(8,128)(2,1)}), bf16[4,16,640]{2,1,0:T(8,128)(2,1)S(1)}, u32[]{:S(2)}, u32[]{:S(2)}) async-start(bf16[4,16,640]{2,1,0:T(8,128)(2,1)} %copy.85), calls=%async_computation | async-start | bytes 163840 | tf_op jit(solution)/shard_map/all_to_all | solution.py:71
  26.3 0.9 concatenate.12
  27.2 42.3 %all_gather.13 = bf16[128,2176]{1,0:T(8,128)(2,1)S(1)} all-gather(bf16[16,2176]{1,0:T(8,128)(2,1)S(1)} %concatenate.12), channel_id=1, replica_groups=mesh['x'=4,'zl'=8,'y'=4,'zh'=2,'core'=2] {'zl'}, dimensions={0}, use_global_device_ids=true | all-gather | bytes 626688 | tf_op jit(solution)/shard_map/all_gather | solution.py:65
  69.5 43.4 %all_gather.12 = bf16[512,640]{1,0:T(8,128)(2,1)S(1)} all-gather(bf16[64,640]{1,0:T(8,128)(2,1)S(1)} %bitcast.41), channel_id=1, replica_groups=mesh['x'=4,'zl'=8,'y'=4,'zh'=2,'core'=2] {'zl'}, dimensions={0}, use_global_device_ids=true | all-gather | bytes 737280 | tf_op jit(solution)/shard_map/all_gather | solution.py:72
  113.1 0.3 copy.90
  113.4 0.1 convert_reduce_fusion
  113.5 0.2 fusion.14
  113.7 0.6 convolution_convert_fusion
  114.3 18.3 %all_to_all.31 = bf16[16,16,2048]{2,1,0:T(8,128)(2,1)S(1)} all-to-all(bf16[16,16,2048]{2,1,0:T(8,128)(2,1)S(1)} %bitcast.36), channel_id=1, replica_groups=mesh['x'=4,'zl'=8,'y'=4,'zh'=2,'core'=2] {'x','y'}, dimensions={0} | all-to-all | bytes 2097152 | tf_op jit(solution)/shard_map/all_to_all | solution.py:81
  132.7 156.0 %all-gather.6.cloned.1.call-done = bf16[1,2048,1536]{2,1,0:T(8,128)(2,1)} async-done(((bf16[1,512,1536]{2,1,0:T(8,128)(2,1)}), bf16[1,2048,1536]{2,1,0:T(8,128)(2,1)}) %all-gather.6.cloned.1.call-update) | async-done | bytes 6291472 | tf_op jit(solution)/shard_map/all_gather | solution.py:77
  288.6 4.6 fusion
  293.2 1.0 fusion.24
  294.2 0.3 copy.87
  294.5 0.1 fusion.32
  294.6 0.7 fusion.13
  295.3 2.0 convolution_convert_fusion.1
  297.4 19.4 %all_to_all.32 = bf16[16,64,512]{2,1,0:T(8,128)(2,1)S(1)} all-to-all(bf16[16,64,512]{2,1,0:T(8,128)(2,1)} %bitcast.39), channel_id=1, replica_groups=mesh['x'=4,'zl'=8,'y'=4,'zh'=2,'core'=2] {'x','y'}, dimensions={0} | all-to-all | bytes 2097152 | tf_op jit(solution)/shard_map/all_to_all | solution.py:87
  316.7 0.4 reshape.253
  317.1 0.7 copy.89
  317.9 0.4 reshape.254
  318.3 37.2 %all-gather.4.cloned.1.call-done = bf16[1024,768]{1,0:T(8,128)(2,1)} async-done(((bf16[256,768]{1,0:T(8,128)(2,1)}), bf16[1024,768]{1,0:T(8,128)(2,1)}) %all-gather.4.cloned.1.call-update) | async-done | bytes 1572880 | tf_op jit(solution)/shard_map/all_gather | solution.py:95
  355.6 3.9 fusion.10
  359.5 0.9 reshape.257
  360.4 0.4 copy.91
  360.8 1.8 all_to_all.25
  362.6 0.6 broadcast.427
  363.2 5.5 %reduce.1 = bf16[512,768]{1,0:T(8,128)(2,1)S(1)} reduce(bf16[512,1,768]{2,1,0:T(2,128)(2,1)S(1)} %all_to_all.25, bf16[]{:T(256)} %broadcast.427), dimensions={1}, to_apply=%all_to_all.25.reduce_sub_computation | reduce | bytes 1572866 | tf_op jit(solution)/shard_map/all_to_all | solution.py:109
  368.7 1.1 reshape.273
  369.7 10.5 %all-to-all-start.3 = ((bf16[512,2,384]{2,1,0:T(2,128)(2,1)}), bf16[512,2,384]{2,1,0:T(2,128)(2,1)S(1)}, u32[]{:S(2)}, u32[]{:S(2)}) async-start(bf16[512,2,384]{2,1,0:T(2,128)(2,1)} %reshape.273), calls=%async_computation.3 | async-start | bytes 1572864 | tf_op jit(solution)/shard_map/all_to_all | solution.py:109
  380.2 46.2 %all-to-all-done.3 = bf16[512,2,384]{2,1,0:T(2,128)(2,1)S(1)} async-done(((bf16[512,2,384]{2,1,0:T(2,128)(2,1)}), bf16[512,2,384]{2,1,0:T(2,128)(2,1)S(1)}, u32[]{:S(2)}, u32[]{:S(2)}) %all-to-all-start.3) | async-done | bytes 786464 | tf_op jit(solution)/shard_map/all_to_all | solution.py:109
  426.5 0.6 reshape.274
  427.1 5.0 %reduce = bf16[512,768]{1,0:T(8,128)(2,1)S(1)} reduce(bf16[512,1,768]{2,1,0:T(2,128)(2,1)S(1)} %reshape.274, bf16[]{:T(256)} %constant.215), dimensions={1}, to_apply=%all_to_all.23.reduce_sub_computation | reduce | bytes 1572866 | tf_op jit(solution)/shard_map/all_to_all | solution.py:109
  432.1 0.5 reshape.258
  432.6 1.0 gather_fusion
  433.6 0.1 bitcast_select_fusion
  433.8 1.2 reduce.2
  435.0 0.6 reshape.275
  435.6 48.3 %all_to_all.33 = bf16[128,2,1536]{2,1,0:T(2,128)(2,1)S(1)} all-to-all(bf16[128,2,1536]{2,1,0:T(2,128)(2,1)S(1)} %reshape.275), channel_id=1, replica_groups=mesh['x'=4,'zl'=8,'y'=4,'zh'=2,'core'=2] {'x','zl','y'}, dimensions={0} | all-to-all | bytes 1572864 | tf_op jit(solution)/shard_map/all_to_all | solution.py:112
  483.8 0.6 reshape.276
  484.5 1.8 copy.94
  486.3 0.7 copy.95
  487.0 0.7 reshape.260
  487.6 1.2 copy.96
  (25 shorter events, 0.2 us)
Async XLA Ops:
  9.7 59.8 %all-to-all-start = ((bf16[4,16,640]{2,1,0:T(8,128)(2,1)}), bf16[4,16,640]{2,1,0:T(8,128)(2,1)S(1)}, u32[]{:S(2)}, u32[]{:S(2)}) async-start(bf16[4,16,640]{2,1,0:T(8,128)(2,1)} %copy.85), calls=%async_computation | async-start | bytes 163840 | tf_op jit(solution)/shard_map/all_to_all | solution.py:71
  26.3 262.3 %all-gather.6.cloned.1.call-start = ((), (), s32[]{:S(2)}) async-start(), calls=%async_computation.6 | async-start | bytes 7864320 | tf_op jit(solution)/shard_map/all_gather | solution.py:77
  113.0 242.6 %all-gather.4.cloned.1.call-start = ((), (), s32[]{:S(2)}) async-start(), calls=%async_computation.5 | async-start | bytes 1966080 | tf_op jit(solution)/shard_map/all_gather | solution.py:95
  317.9 37.7 %copy-start = (bf16[1,512,768]{2,1,0:T(8,128)(2,1)S(1)}, bf16[1,512,768]{2,1,0:T(8,128)(2,1)}, u32[]{:S(2)}) copy-start(bf16[1,512,768]{2,1,0:T(8,128)(2,1)} %param.16) | copy-start | bytes 2359300
  368.6 11.6 %copy-start.1 = (s32[128]{0:T(128)S(1)}, s32[128]{0:T(128)}, u32[]{:S(2)}) copy-start(s32[128]{0:T(128)} %param.17) | copy-start | bytes 1540
  369.7 56.8 %all-to-all-start.3 = ((bf16[512,2,384]{2,1,0:T(2,128)(2,1)}), bf16[512,2,384]{2,1,0:T(2,128)(2,1)S(1)}, u32[]{:S(2)}, u32[]{:S(2)}) async-start(bf16[512,2,384]{2,1,0:T(2,128)(2,1)} %reshape.273), calls=%async_computation.3 | async-start | bytes 1572864 | tf_op jit(solution)/shard_map/all_to_all | solution.py:109
Sparse Core Ops, SparseCore 0:
  113.1 175.4 all-gather.5
  294.3 61.2 all-gather.3

commit v2 on v1

--- a/solution.py
+++ b/solution.py
@@ -73,7 +73,6 @@
         cot_parts.reshape(groups * tok_rows, share + META), "zl", axis=0, tiled=True
     )
 
-    gate_up, cot_pack, tok_pack = lax.optimization_barrier((gate_up, cot_pack, tok_pack))
     weights = lax.all_gather(gate_up[0], DP, axis=0, tiled=True)
 
     tok_pick, _ = pickers(tok_pack[:, width:], line, tok_rows, top)

time: 496 us -> 448 us (0.903)
  waiting for transfers between devices: 239 us -> 77.2 us
  starting transfers between devices: 27.1 us -> 103 us
  blocking collectives: 172 us -> 212 us
    all_gather x1, waiting for transfers between devices: 156 us -> 18.9 us  [shards(): weights = lax.all_gather(gate_up[0], DP, axis=0, tiled=True)]
    all_to_all x1, starting transfers between devices: 16.6 us -> 78.6 us  [shards(): lax.all_to_all(cot_parts, DP, split_axis=0, concat_axis=0, tiled=True)]
    all_gather x1, waiting for transfers between devices: 37.2 us -> 0.02 us  [shards(): hidden = lax.all_gather(hidden, DP, axis=0, tiled=True)]
    all_gather x1, blocking collectives: 43.4 us -> 79.7 us  [shards(): lax.all_gather(cot_parts.reshape(groups * tok_rows, share + META), 'zl',...]
    all_gather x1, blocking collectives: 42.3 us -> 63.2 us  [shards(): lax.all_gather(jnp.concatenate([tokens, meta], axis=1), 'zl', axis=0, til...]
    all_to_all x1 -> x0, blocking collectives: 18.3 us -> none  [shards(): lax.all_to_all(rows.reshape(plane, line * CAP, width), PLANE, split_axis=...]
    all_to_all x0 -> x1, waiting for transfers between devices: none -> 11.3 us  [shards(): lax.all_to_all(rows.reshape(plane, line * CAP, width), PLANE, split_axis=...]
    all_to_all x1, starting transfers between devices: 10.5 us -> 18.7 us  [shards(): lax.all_to_all(pieces, EXPERT + DP, split_axis=0, concat_axis=0, tiled=True)]
  transfers between devices with their start and end apart: 4 -> 5, of which waited for: 3 -> 3; matrix products, arithmetic and copies ran while one was open for 1% -> 3% of each run, Pallas kernels for 0% -> 0%
where the time goes in v2:
time: 448 us
  blocking collectives  212 us (47%)
  starting transfers between devices  103 us (23%)
  waiting for transfers between devices  77.2 us (17%)
  local copies, waits for them, and re-layouts  15.9 us (4%)
  between operations  13.7 us (3%)
  other arithmetic  13.1 us (3%)
  matrix products  13 us (3%)
    all_gather x1, blocking collectives, shards(): lax.all_gather(cot_parts.reshape(groups * tok_rows, share + META), 'zl',...  79.7 us
    all_to_all x1, starting transfers between devices, shards(): lax.all_to_all(cot_parts, DP, split_axis=0, concat_axis=0, tiled=True)  78.6 us
    all_gather x1, blocking collectives, shards(): lax.all_gather(jnp.concatenate([tokens, meta], axis=1), 'zl', axis=0, til...  63.2 us
    all_to_all x1, blocking collectives, shards(): lax.all_to_all(picked, EXPERT, split_axis=0, concat_axis=0, tiled=True)  48.3 us
    all_to_all x1, waiting for transfers between devices, shards(): lax.all_to_all(pieces, EXPERT + DP, split_axis=0, concat_axis=0, tiled=True)  46.2 us
    all_to_all x1, blocking collectives, shards(): lax.all_to_all(scaled.reshape(plane, line * groups * CAP, share), PLANE,...  20.4 us
    all_gather x1, waiting for transfers between devices, shards(): weights = lax.all_gather(gate_up[0], DP, axis=0, tiled=True)  18.9 us
    all_to_all x1, starting transfers between devices, shards(): lax.all_to_all(pieces, EXPERT + DP, split_axis=0, concat_axis=0, tiled=True)  18.7 us
  transfers between devices with their start and end apart: 5, of which 3 were waited for; matrix products, arithmetic and copies ran while one was open for 3% of the time, Pallas kernels for 0%

profile of v2, /device:TPU:1, one launch (start us, length us, event | category | flops | bytes accessed | tf_op | source)
XLA Modules:
  0.0 447.6 jit_solution(951209966834745455)
XLA Ops:
  6.5 0.7 all-gather.6.cloned.1.call-update
  7.3 0.1 copy.84
  7.4 0.1 concatenate.12
  7.5 63.2 %all_gather.13 = bf16[128,2176]{1,0:T(8,128)(2,1)S(1)} all-gather(bf16[16,2176]{1,0:T(8,128)(2,1)S(1)} %concatenate.12), channel_id=1, replica_groups=mesh['x'=4,'zl'=8,'y'=4,'zh'=2,'core'=2] {'zl'}, dimensions={0}, use_global_device_ids=true | all-gather | bytes 626688 | tf_op jit(solution)/shard_map/all_gather | solution.py:65
  70.9 0.1 convert_reduce_fusion
  71.0 0.2 fusion.14
  71.2 1.6 convolution_convert_fusion
  72.8 5.8 %all-to-all-start.2 = ((bf16[16,16,2048]{2,1,0:T(8,128)(2,1)}), bf16[16,16,2048]{2,1,0:T(8,128)(2,1)S(1)}, u32[]{:S(2)}, u32[]{:S(2)}) async-start(bf16[16,16,2048]{2,1,0:T(8,128)(2,1)} %bitcast.6), calls=%async_computation.2 | async-start | bytes 2097152 | tf_op jit(solution)/shard_map/all_to_all | solution.py:80
  78.7 0.1 pad_maximum_fusion.1
  78.8 0.6 copy.85
  79.5 11.3 %all-to-all-done.2 = bf16[16,16,2048]{2,1,0:T(8,128)(2,1)S(1)} async-done(((bf16[16,16,2048]{2,1,0:T(8,128)(2,1)}), bf16[16,16,2048]{2,1,0:T(8,128)(2,1)S(1)}, u32[]{:S(2)}, u32[]{:S(2)}) %all-to-all-start.2) | async-done | bytes 1048608 | tf_op jit(solution)/shard_map/all_to_all | solution.py:80
  90.8 78.6 %all-to-all-start = ((bf16[4,16,640]{2,1,0:T(8,128)(2,1)}), bf16[4,16,640]{2,1,0:T(8,128)(2,1)S(1)}, u32[]{:S(2)}, u32[]{:S(2)}) async-start(bf16[4,16,640]{2,1,0:T(8,128)(2,1)} %copy.85), calls=%async_computation | async-start | bytes 163840 | tf_op jit(solution)/shard_map/all_to_all | solution.py:71
  169.4 18.9 %all-gather.6.cloned.1.call-done = bf16[1,2048,1536]{2,1,0:T(8,128)(2,1)} async-done(((bf16[1,512,1536]{2,1,0:T(8,128)(2,1)}), bf16[1,2048,1536]{2,1,0:T(8,128)(2,1)}) %all-gather.6.cloned.1.call-update) | async-done | bytes 6291472 | tf_op jit(solution)/shard_map/all_gather | solution.py:76
  188.3 4.6 %fusion = f32[256,1536]{1,0:T(8,128)S(1)} fusion(bf16[256,2048]{1,0:T(8,128)(2,1)S(1)} %bitcast.38, bf16[1,2048,1536]{2,1,0:T(8,128)(2,1)} %all-gather.6.cloned.1.call-done), kind=kOutput, calls=%fused_computation.1 | convolution fusion | flops 1610612736 | bytes 8912896 | tf_op jit(solution)/shard_map/dot_general | solution.py:92
  192.9 1.0 fusion.24
  193.9 79.7 %all_gather.12 = bf16[512,640]{1,0:T(8,128)(2,1)S(1)} all-gather(bf16[64,640]{1,0:T(8,128)(2,1)S(1)} %bitcast.40), channel_id=1, replica_groups=mesh['x'=4,'zl'=8,'y'=4,'zh'=2,'core'=2] {'zl'}, dimensions={0}, use_global_device_ids=true | all-gather | bytes 737280 | tf_op jit(solution)/shard_map/all_gather | solution.py:72
  273.6 0.1 fusion.81
  273.8 0.1 copy.98
  273.9 0.1 fusion.32
  274.0 0.7 fusion.13
  274.7 2.0 convolution_convert_fusion.1
  276.8 20.4 %all_to_all.31 = bf16[16,64,512]{2,1,0:T(8,128)(2,1)S(1)} all-to-all(bf16[16,64,512]{2,1,0:T(8,128)(2,1)} %bitcast.39), channel_id=1, replica_groups=mesh['x'=4,'zl'=8,'y'=4,'zh'=2,'core'=2] {'x','y'}, dimensions={0} | all-to-all | bytes 2097152 | tf_op jit(solution)/shard_map/all_to_all | solution.py:86
  297.1 0.4 reshape.253
  297.6 0.7 copy.88
  298.3 0.4 reshape.254
  298.8 0.6 copy-done.4
  299.4 3.9 fusion.10
  303.3 0.9 reshape.257
  304.2 0.4 copy.91
  304.6 1.8 all_to_all.25
  306.4 0.5 broadcast.427
  306.9 5.4 %reduce.1 = bf16[512,768]{1,0:T(8,128)(2,1)S(1)} reduce(bf16[512,1,768]{2,1,0:T(2,128)(2,1)S(1)} %all_to_all.25, bf16[]{:T(256)} %broadcast.427), dimensions={1}, to_apply=%all_to_all.25.reduce_sub_computation | reduce | bytes 1572866 | tf_op jit(solution)/shard_map/all_to_all | solution.py:108
  312.4 1.1 reshape.273
  313.4 18.7 %all-to-all-start.3 = ((bf16[512,2,384]{2,1,0:T(2,128)(2,1)}), bf16[512,2,384]{2,1,0:T(2,128)(2,1)S(1)}, u32[]{:S(2)}, u32[]{:S(2)}) async-start(bf16[512,2,384]{2,1,0:T(2,128)(2,1)} %reshape.273), calls=%async_computation.3 | async-start | bytes 1572864 | tf_op jit(solution)/shard_map/all_to_all | solution.py:108
  332.2 46.2 %all-to-all-done.3 = bf16[512,2,384]{2,1,0:T(2,128)(2,1)S(1)} async-done(((bf16[512,2,384]{2,1,0:T(2,128)(2,1)}), bf16[512,2,384]{2,1,0:T(2,128)(2,1)S(1)}, u32[]{:S(2)}, u32[]{:S(2)}) %all-to-all-start.3) | async-done | bytes 786464 | tf_op jit(solution)/shard_map/all_to_all | solution.py:108
  378.4 0.6 reshape.274
  379.1 5.0 %reduce = bf16[512,768]{1,0:T(8,128)(2,1)S(1)} reduce(bf16[512,1,768]{2,1,0:T(2,128)(2,1)S(1)} %reshape.274, bf16[]{:T(256)} %constant.215), dimensions={1}, to_apply=%all_to_all.23.reduce_sub_computation | reduce | bytes 1572866 | tf_op jit(solution)/shard_map/all_to_all | solution.py:108
  384.1 0.5 reshape.258
  384.5 1.0 gather_fusion
  385.6 0.1 bitcast_select_fusion
  385.7 1.2 reduce.2
  386.9 0.6 reshape.275
  387.5 48.3 %all_to_all.32 = bf16[128,2,1536]{2,1,0:T(2,128)(2,1)S(1)} all-to-all(bf16[128,2,1536]{2,1,0:T(2,128)(2,1)S(1)} %reshape.275), channel_id=1, replica_groups=mesh['x'=4,'zl'=8,'y'=4,'zh'=2,'core'=2] {'x','zl','y'}, dimensions={0} | all-to-all | bytes 1572864 | tf_op jit(solution)/shard_map/all_to_all | solution.py:111
  435.7 0.6 reshape.276
  436.4 1.8 copy.94
  438.1 0.7 copy.95
  438.9 0.7 reshape.260
  439.5 1.2 copy.96
  (38 shorter events, 0.5 us)
Async XLA Ops:
  6.5 0.7 copy-start.3
  6.5 0.8 copy-start.2
  6.5 0.9 copy-start
  6.5 181.8 %all-gather.6.cloned.1.call-start = ((), (), s32[]{:S(2)}) async-start(), calls=%async_computation.6 | async-start | bytes 7864320 | tf_op jit(solution)/shard_map/all_gather | solution.py:76
  71.2 7.5 %copy-start.1 = (bf16[16,2048]{1,0:T(8,128)(2,1)S(1)}, bf16[16,2048]{1,0:T(8,128)(2,1)}, u32[]{:S(2)}) copy-start(bf16[16,2048]{1,0:T(8,128)(2,1)} %param.10) | copy-start | bytes 196612
  72.8 18.0 %all-to-all-start.2 = ((bf16[16,16,2048]{2,1,0:T(8,128)(2,1)}), bf16[16,16,2048]{2,1,0:T(8,128)(2,1)S(1)}, u32[]{:S(2)}, u32[]{:S(2)}) async-start(bf16[16,16,2048]{2,1,0:T(8,128)(2,1)} %bitcast.6), calls=%async_computation.2 | async-start | bytes 2097152 | tf_op jit(solution)/shard_map/all_to_all | solution.py:80
  90.8 103.1 %all-to-all-start = ((bf16[4,16,640]{2,1,0:T(8,128)(2,1)}), bf16[4,16,640]{2,1,0:T(8,128)(2,1)S(1)}, u32[]{:S(2)}, u32[]{:S(2)}) async-start(bf16[4,16,640]{2,1,0:T(8,128)(2,1)} %copy.85), calls=%async_computation | async-start | bytes 163840 | tf_op jit(solution)/shard_map/all_to_all | solution.py:71
  169.4 129.4 %all-gather.4.cloned.1.call-start = ((), (), s32[]{:S(2)}) async-start(), calls=%async_computation.5 | async-start | bytes 1966080 | tf_op jit(solution)/shard_map/all_gather | solution.py:94
  298.3 1.1 copy-start.4
  312.3 19.8 %copy-start.5 = (s32[128]{0:T(128)S(1)}, s32[128]{0:T(128)}, u32[]{:S(2)}) copy-start(s32[128]{0:T(128)} %param.17) | copy-start | bytes 1540
  313.4 65.0 %all-to-all-start.3 = ((bf16[512,2,384]{2,1,0:T(2,128)(2,1)}), bf16[512,2,384]{2,1,0:T(2,128)(2,1)S(1)}, u32[]{:S(2)}, u32[]{:S(2)}) async-start(bf16[512,2,384]{2,1,0:T(2,128)(2,1)} %reshape.273), calls=%async_computation.3 | async-start | bytes 1572864 | tf_op jit(solution)/shard_map/all_to_all | solution.py:108
Sparse Core Ops, SparseCore 0:
  9.4 178.8 all-gather.5
  194.0 86.3 all-gather.3

commit v3 on v2

--- a/solution.py
+++ b/solution.py
@@ -1,6 +1,8 @@
 import jax
 import jax.numpy as jnp
 from jax import lax
+from jax.experimental import pallas as pl
+from jax.experimental.pallas import tpu as pltpu
 from jax.sharding import Mesh, PartitionSpec as P
 
 OPT_STEP = 2
@@ -18,6 +20,131 @@
 META = 128
 
 contract_rows = (((0,), (0,)), ((), ()))
+
+
+LINE = 8
+MESH = pl.DeviceIdType.MESH
+
+
+def line_gather_kernel(
+    tok_ref, cot_ref, tok_all, cot_all, tok_recv, tok_send, cot_recv, cot_send, dp_recv, dp_send, own_sem
+):
+    at, zh, core = lax.axis_index("zl"), lax.axis_index("zh"), lax.axis_index("core")
+    me = zh * 2 + core
+    has = (at < LINE - 1, at > 0)
+    ids = ({"zl": jnp.minimum(at + 1, LINE - 1)}, {"zl": jnp.maximum(at - 1, 0)})
+    partners = []
+    for dz, dc in ((0, 1), (1, 0), (1, 1)):
+        partners.append(((zh + dz) % 2, (core + dc) % 2))
+
+    barrier = pltpu.get_barrier_semaphore()
+    for far in (0, 1):
+
+        @pl.when(has[far])
+        def _():
+            pl.semaphore_signal(barrier, inc=1, device_id=ids[far], device_id_type=MESH)
+
+    for pz, pc in partners:
+        pl.semaphore_signal(barrier, inc=1, device_id={"zh": pz, "core": pc}, device_id_type=MESH)
+    pl.semaphore_wait(barrier, 3 + has[0].astype(jnp.int32) + has[1].astype(jnp.int32))
+
+    def hop(out, recv, send, block, far, source=None):
+        return pltpu.make_async_remote_copy(
+            src_ref=out.at[block] if source is None else source,
+            dst_ref=out.at[block],
+            send_sem=send.at[far, block],
+            recv_sem=recv.at[block],
+            device_id=ids[far],
+            device_id_type=MESH,
+        )
+
+    def first(out, recv, send, source=None):
+        for far in (0, 1):
+
+            @pl.when(has[far])
+            def _():
+                hop(out, recv, send, at, far, source).start()
+
+    def step(out, recv, send, s):
+        for far in (0, 1):
+            block = at - s if far == 0 else at + s
+            there = block >= 0 if far == 0 else block < LINE
+
+            @pl.when(there)
+            def _():
+                hop(out, recv, send, block, far).wait_recv()
+
+            @pl.when(there & has[far])
+            def _():
+                hop(out, recv, send, block, far).start()
+
+    def finish(out, recv, send, source=None):
+        for s in range(LINE):
+            for far in (0, 1):
+                block = at - s if far == 0 else at + s
+                there = block >= 0 if far == 0 else block < LINE
+
+                @pl.when(there & has[far])
+                def _():
+                    hop(out, recv, send, block, far, source if s == 0 else None).wait_send()
+
+    own_tok = pltpu.make_async_copy(tok_ref, tok_all.at[at], own_sem.at[0])
+    own_cot = pltpu.make_async_copy(cot_ref.at[me], cot_all.at[at, me], own_sem.at[1])
+    swaps = [
+        pltpu.make_async_remote_copy(
+            src_ref=cot_ref.at[pz * 2 + pc],
+            dst_ref=cot_all.at[at, me],
+            send_sem=dp_send.at[k],
+            recv_sem=dp_recv.at[k],
+            device_id={"zh": pz, "core": pc},
+            device_id_type=MESH,
+        )
+        for k, (pz, pc) in enumerate(partners)
+    ]
+    tok = (tok_all, tok_recv, tok_send)
+    cot = (cot_all, cot_recv, cot_send)
+    for swap in swaps:
+        swap.start()
+    first(*tok, tok_ref)
+    own_tok.start()
+    own_cot.start()
+    lead = 3
+    for s in range(1, lead):
+        step(*tok, s)
+    for swap in swaps:
+        swap.wait()
+    own_cot.wait()
+    first(*cot)
+    for s in range(lead, LINE + lead - 1):
+        if s < LINE:
+            step(*tok, s)
+        step(*cot, s - lead + 1)
+    own_tok.wait()
+    finish(*tok, tok_ref)
+    finish(*cot)
+
+
+def line_gather(tok, cot):
+    dma = pltpu.SemaphoreType.DMA
+    return pl.pallas_call(
+        line_gather_kernel,
+        out_shape=(
+            jax.ShapeDtypeStruct((LINE,) + tok.shape, tok.dtype),
+            jax.ShapeDtypeStruct((LINE,) + cot.shape, cot.dtype),
+        ),
+        in_specs=[pl.BlockSpec(memory_space=pltpu.VMEM)] * 2,
+        out_specs=(pl.BlockSpec(memory_space=pltpu.VMEM),) * 2,
+        scratch_shapes=[
+            dma((LINE,)),
+            dma((2, LINE)),
+            dma((LINE,)),
+            dma((2, LINE)),
+            dma((3,)),
+            dma((3,)),
+            dma((2,)),
+        ],
+        compiler_params=pltpu.CompilerParams(collective_id=0, has_side_effects=True),
+    )(tok, cot)
 
 
 def pickers(meta, blocks, block_rows, top):
@@ -62,21 +189,20 @@
     meta = jnp.concatenate(
         [route_ids.astype(bf16), route_gates, jnp.zeros((tok_rows, META - 2 * top), bf16)], axis=1
     )
-    tok_pack = lax.all_gather(jnp.concatenate([tokens, meta], axis=1), "zl", axis=0, tiled=True)
-
     cot_parts = cotangent.reshape(tok_rows, groups, share).transpose(1, 0, 2)
     cot_parts = jnp.concatenate(
         [cot_parts, jnp.broadcast_to(meta[None], (groups, tok_rows, META))], axis=2
     )
-    cot_parts = lax.all_to_all(cot_parts, DP, split_axis=0, concat_axis=0, tiled=True)
-    cot_pack = lax.all_gather(
-        cot_parts.reshape(groups * tok_rows, share + META), "zl", axis=0, tiled=True
-    )
-
+    tok_line, cot_line = line_gather(tokens, cot_parts)
+    gate_up, tok_line, cot_line = lax.optimization_barrier((gate_up, tok_line, cot_line))
+    tok_line = tok_line.reshape(line * tok_rows, width)
+    own_meta = lax.dynamic_index_in_dim(cot_line[:, :, :, share:], lax.axis_index(DP), 1, keepdims=False)
+    own_meta = own_meta.reshape(line * tok_rows, META)
+    cot_pack = cot_line.reshape(line * groups * tok_rows, share + META)
     weights = lax.all_gather(gate_up[0], DP, axis=0, tiled=True)
 
-    tok_pick, _ = pickers(tok_pack[:, width:], line, tok_rows, top)
-    rows = jnp.dot(tok_pick, tok_pack[:, :width], preferred_element_type=jnp.float32).astype(bf16)
+    tok_pick, _ = pickers(own_meta, line, tok_rows, top)
+    rows = jnp.dot(tok_pick, tok_line, preferred_element_type=jnp.float32).astype(bf16)
     rows = lax.all_to_all(
         rows.reshape(plane, line * CAP, width), PLANE, split_axis=0, concat_axis=0, tiled=True
     ).reshape(plane * line * CAP, width)
@@ -89,6 +215,7 @@
     scaled = scaled.reshape(plane * line, groups, CAP, share).transpose(1, 0, 2, 3)
     scaled = scaled.reshape(groups * plane * line * CAP, share)
 
+    weights, scaled = lax.optimization_barrier((weights, scaled))
     pre = jnp.dot(rows, weights, preferred_element_type=jnp.float32)
     hidden = (jax.nn.silu(pre[:, :hidden_units]) * pre[:, hidden_units:]).astype(bf16)
     hidden = lax.all_gather(hidden, DP, axis=0, tiled=True)

time: 448 us -> 429 us (0.958)
  waiting for transfers between devices: 77.2 us -> 250 us
  blocking collectives: 212 us -> 48.3 us
  starting transfers between devices: 103 us -> 21.2 us
  Pallas kernels: 0 us -> 49.9 us
    all_gather x2 -> x0, blocking collectives: 143 us -> none  [the longest x1 79.7 us: shards(): lax.all_gather(cot_parts.reshape(groups * tok_rows, share + META), 'zl',...]
    all_gather x1, waiting for transfers between devices: 18.9 us -> 133 us  [shards(): weights = lax.all_gather(gate_up[0], DP, axis=0, tiled=True)]
    all_to_all x1, starting transfers between devices: 78.6 us -> 6.89 us  [shards(): lax.all_to_all(scaled.reshape(plane, line * groups * CAP, share), PLANE,...]
    all_gather x1, waiting for transfers between devices: 0.02 us -> 61.4 us  [shards(): hidden = lax.all_gather(hidden, DP, axis=0, tiled=True)]
    pallas_call x0 -> x1, Pallas kernels: none -> 49.9 us  [line_gather(): pl.pallas_call(line_gather_kernel, out_shape=(jax.ShapeDtypeStruct((LINE,...]
    all_to_all x1 -> x0, blocking collectives: 20.4 us -> none  [shards(): lax.all_to_all(scaled.reshape(plane, line * groups * CAP, share), PLANE,...]
    all_to_all x1, waiting for transfers between devices: 11.3 us -> 0.01 us  [shards(): lax.all_to_all(rows.reshape(plane, line * CAP, width), PLANE, split_axis=...]
    all_to_all x1, waiting for transfers between devices: 0.01 us -> 9.79 us  [shards(): lax.all_to_all(scaled.reshape(plane, line * groups * CAP, share), PLANE,...]
  transfers between devices with their start and end apart: 5 -> 5, of which waited for: 3 -> 4; matrix products, arithmetic and copies ran while one was open for 3% -> 2% of each run, Pallas kernels for 0% -> 0%
where the time goes in v3:
time: 429 us; the launch traced here: 428 us
  waiting for transfers between devices  250 us (58%)
  Pallas kernels  49.9 us (12%)
  blocking collectives  48.3 us (11%)
  starting transfers between devices  21.2 us (5%)
  local copies, waits for them, and re-layouts  17.2 us (4%)
  other arithmetic  14.1 us (3%)
  between operations  13.7 us (3%)
  matrix products  13 us (3%)
    all_gather x1, waiting for transfers between devices, shards(): weights = lax.all_gather(gate_up[0], DP, axis=0, tiled=True)  133 us
    all_gather x1, waiting for transfers between devices, shards(): hidden = lax.all_gather(hidden, DP, axis=0, tiled=True)  61.4 us
    pallas_call x1, Pallas kernels, line_gather(): pl.pallas_call(line_gather_kernel, out_shape=(jax.ShapeDtypeStruct((LINE,...  49.9 us
    all_to_all x1, blocking collectives, shards(): lax.all_to_all(picked, EXPERT, split_axis=0, concat_axis=0, tiled=True)  48.3 us
    all_to_all x1, waiting for transfers between devices, shards(): lax.all_to_all(pieces, EXPERT + DP, split_axis=0, concat_axis=0, tiled=True)  46.2 us
    all_to_all x1, starting transfers between devices, shards(): lax.all_to_all(pieces, EXPERT + DP, split_axis=0, concat_axis=0, tiled=True)  10.5 us
    all_to_all x2, other arithmetic, shards(): lax.all_to_all(pieces, EXPERT + DP, split_axis=0, concat_axis=0, tiled=True)  10.2 us
    all_to_all x1, waiting for transfers between devices, shards(): lax.all_to_all(scaled.reshape(plane, line * groups * CAP, share), PLANE,...  9.79 us
  transfers between devices with their start and end apart: 5, of which 4 were waited for; matrix products, arithmetic and copies ran while one was open for 2% of the time, Pallas kernels for 0%

profile of v3, /device:TPU:1, one launch (start us, length us, event | category | flops | bytes accessed | tf_op | source)
XLA Modules:
  0.0 427.9 jit_solution(17678381092717206036)
XLA Ops:
  6.5 0.8 copy.91
  7.4 0.7 convert_element_type.86
  8.1 0.1 copy.74
  8.2 0.8 copy.75
  9.0 0.1 maximum_maximum_fusion
  9.1 0.6 pad_maximum_fusion.cot_ref
  9.7 49.9 %shard_map.91 = (bf16[8,16,2048]{2,1,0:T(8,128)(2,1)}, bf16[8,4,16,640]{3,2,1,0:T(8,128)(2,1)}) custom-call(bf16[16,2048]{1,0:T(8,128)(2,1)} %tok_ref.1, bf16[4,16,640]{2,1,0:T(8,128)(2,1)} %pad_maximum_fusion.cot_ref), custom_call_target="tpu_custom_call" | custom-call | tf_op jit(solution)/shard_map/pallas_call | solution.py:129
  59.7 1.1 copy-done.1
  60.8 0.1 fusion.78
  61.0 0.1 copy.87
  61.1 0.1 fusion.29
  61.2 0.7 fusion.11
  61.9 2.0 convolution_convert_fusion.1
  64.0 6.9 %all-to-all-start = ((bf16[16,64,512]{2,1,0:T(8,128)(2,1)}), bf16[16,64,512]{2,1,0:T(8,128)(2,1)S(1)}, u32[]{:S(2)}, u32[]{:S(2)}) async-start(bf16[16,64,512]{2,1,0:T(8,128)(2,1)} %bitcast.5), calls=%async_computation | async-start | bytes 2097152 | tf_op jit(solution)/shard_map/all_to_all | solution.py:212
  71.1 0.2 fusion.12
  71.3 1.6 convolution_convert_fusion
  72.9 9.8 %all-to-all-done = bf16[16,64,512]{2,1,0:T(8,128)(2,1)S(1)} async-done(((bf16[16,64,512]{2,1,0:T(8,128)(2,1)}), bf16[16,64,512]{2,1,0:T(8,128)(2,1)S(1)}, u32[]{:S(2)}, u32[]{:S(2)}) %all-to-all-start) | async-done | bytes 1048608 | tf_op jit(solution)/shard_map/all_to_all | solution.py:212
  82.7 3.7 all-to-all-start.1
  86.4 0.2 all-gather.4.cloned.1.call-start
  86.6 0.4 reshape.260
  87.1 0.7 copy.78
  87.8 0.4 reshape.261
  88.2 133.0 %all-gather.6.cloned.1.call-done = bf16[1,2048,1536]{2,1,0:T(8,128)(2,1)} async-done(((bf16[1,512,1536]{2,1,0:T(8,128)(2,1)}), bf16[1,2048,1536]{2,1,0:T(8,128)(2,1)}) %all-gather.6.cloned.1.call-update) | async-done | bytes 6291472 | tf_op jit(solution)/shard_map/all_gather | solution.py:202
  221.2 4.6 %fusion.79 = f32[256,1536]{1,0:T(8,128)S(1)} fusion(bf16[256,2048]{1,0:T(8,128)(2,1)S(1)} %bitcast.47, bf16[2048,1536]{1,0:T(8,128)(2,1)} %bitcast.54), kind=kOutput, calls=%fused_computation.128 | convolution fusion | flops 1610612736 | bytes 8912896 | tf_op jit(solution)/shard_map/dot_general | solution.py:219
  225.8 1.0 fusion.22
  226.8 61.4 %all-gather.4.cloned.1.call-done = bf16[1024,768]{1,0:T(8,128)(2,1)} async-done(((bf16[256,768]{1,0:T(8,128)(2,1)}), bf16[1024,768]{1,0:T(8,128)(2,1)}) %all-gather.4.cloned.1.call-update) | async-done | bytes 1572880 | tf_op jit(solution)/shard_map/all_gather | solution.py:221
  288.2 3.9 fusion.8
  292.1 0.9 reshape.266
  293.0 0.4 copy.80
  293.4 1.8 all_to_all.21
  295.2 0.5 broadcast.429
  295.7 5.4 %reduce.1 = bf16[512,768]{1,0:T(8,128)(2,1)S(1)} reduce(bf16[512,1,768]{2,1,0:T(2,128)(2,1)S(1)} %all_to_all.21, bf16[]{:T(256)} %broadcast.429), dimensions={1}, to_apply=%all_to_all.21.reduce_sub_computation | reduce | bytes 1572866 | tf_op jit(solution)/shard_map/all_to_all | solution.py:235
  301.1 1.1 reshape.282
  302.2 10.5 %all-to-all-start.2 = ((bf16[512,2,384]{2,1,0:T(2,128)(2,1)}), bf16[512,2,384]{2,1,0:T(2,128)(2,1)S(1)}, u32[]{:S(2)}, u32[]{:S(2)}) async-start(bf16[512,2,384]{2,1,0:T(2,128)(2,1)} %reshape.282), calls=%async_computation.2 | async-start | bytes 1572864 | tf_op jit(solution)/shard_map/all_to_all | solution.py:235
  312.7 46.2 %all-to-all-done.2 = bf16[512,2,384]{2,1,0:T(2,128)(2,1)S(1)} async-done(((bf16[512,2,384]{2,1,0:T(2,128)(2,1)}), bf16[512,2,384]{2,1,0:T(2,128)(2,1)S(1)}, u32[]{:S(2)}, u32[]{:S(2)}) %all-to-all-start.2) | async-done | bytes 786464 | tf_op jit(solution)/shard_map/all_to_all | solution.py:235
  358.9 0.6 reshape.283
  359.6 4.8 %reduce = bf16[512,768]{1,0:T(8,128)(2,1)S(1)} reduce(bf16[512,1,768]{2,1,0:T(2,128)(2,1)S(1)} %reshape.283, bf16[]{:T(256)} %constant.225), dimensions={1}, to_apply=%all_to_all.19.reduce_sub_computation | reduce | bytes 1572866 | tf_op jit(solution)/shard_map/all_to_all | solution.py:235
  364.4 0.5 reshape.267
  364.9 1.0 gather_fusion
  365.9 0.1 bitcast_select_fusion
  366.0 1.1 reduce.2
  367.2 0.6 reshape.284
  367.8 48.3 %all_to_all.26 = bf16[128,2,1536]{2,1,0:T(2,128)(2,1)S(1)} all-to-all(bf16[128,2,1536]{2,1,0:T(2,128)(2,1)S(1)} %reshape.284), channel_id=1, replica_groups=mesh['x'=4,'zl'=8,'y'=4,'zh'=2,'core'=2] {'x','zl','y'}, dimensions={0} | all-to-all | bytes 1572864 | tf_op jit(solution)/shard_map/all_to_all | solution.py:238
  416.0 0.6 reshape.285
  416.7 1.8 copy.83
  418.4 0.7 copy.84
  419.2 0.7 reshape.269
  419.8 1.2 copy.85
  (32 shorter events, 0.5 us)
Async XLA Ops:
  6.5 214.7 %all-gather.6.cloned.1.call-start = ((), (), s32[]{:S(2)}) async-start(), calls=%async_computation.5 | async-start | bytes 7864320 | tf_op jit(solution)/shard_map/all_gather | solution.py:202
  59.7 1.1 copy-start.1
  64.0 7.4 %copy-start = (bf16[8,16,2048]{2,1,0:T(8,128)(2,1)S(1)}, bf16[8,16,2048]{2,1,0:T(8,128)(2,1)}, u32[]{:S(2)}) copy-start(bf16[8,16,2048]{2,1,0:T(8,128)(2,1)} %get-tuple-element.17) | copy-start | bytes 1572868
  64.0 18.8 %all-to-all-start = ((bf16[16,64,512]{2,1,0:T(8,128)(2,1)}), bf16[16,64,512]{2,1,0:T(8,128)(2,1)S(1)}, u32[]{:S(2)}, u32[]{:S(2)}) async-start(bf16[16,64,512]{2,1,0:T(8,128)(2,1)} %bitcast.5), calls=%async_computation | async-start | bytes 2097152 | tf_op jit(solution)/shard_map/all_to_all | solution.py:212
  82.7 138.5 %all-to-all-start.1 = ((bf16[16,16,2048]{2,1,0:T(8,128)(2,1)}), bf16[16,16,2048]{2,1,0:T(8,128)(2,1)S(1)}, u32[]{:S(2)}, u32[]{:S(2)}) async-start(bf16[16,16,2048]{2,1,0:T(8,128)(2,1)} %bitcast.9), calls=%async_computation.1 | async-start | bytes 2097152 | tf_op jit(solution)/shard_map/all_to_all | solution.py:206
  86.4 201.8 %all-gather.4.cloned.1.call-start = ((), (), s32[]{:S(2)}) async-start(), calls=%async_computation.4 | async-start | bytes 1966080 | tf_op jit(solution)/shard_map/all_gather | solution.py:221
  225.8 62.4 %copy-start.2 = (bf16[1,512,768]{2,1,0:T(8,128)(2,1)S(1)}, bf16[1,512,768]{2,1,0:T(8,128)(2,1)}, u32[]{:S(2)}) copy-start(bf16[1,512,768]{2,1,0:T(8,128)(2,1)} %param.16) | copy-start | bytes 2359300
  301.1 11.6 %copy-start.3 = (s32[128]{0:T(128)S(1)}, s32[128]{0:T(128)}, u32[]{:S(2)}) copy-start(s32[128]{0:T(128)} %param.17) | copy-start | bytes 1540
  302.2 56.8 %all-to-all-start.2 = ((bf16[512,2,384]{2,1,0:T(2,128)(2,1)}), bf16[512,2,384]{2,1,0:T(2,128)(2,1)S(1)}, u32[]{:S(2)}, u32[]{:S(2)}) async-start(bf16[512,2,384]{2,1,0:T(2,128)(2,1)} %reshape.282), calls=%async_computation.2 | async-start | bytes 1572864 | tf_op jit(solution)/shard_map/all_to_all | solution.py:235
Sparse Core Ops, SparseCore 0:
  59.8 161.3 all-gather.5
  226.9 61.2 all-gather.3

commit v4 on v3

--- a/solution.py
+++ b/solution.py
@@ -194,7 +194,6 @@
         [cot_parts, jnp.broadcast_to(meta[None], (groups, tok_rows, META))], axis=2
     )
     tok_line, cot_line = line_gather(tokens, cot_parts)
-    gate_up, tok_line, cot_line = lax.optimization_barrier((gate_up, tok_line, cot_line))
     tok_line = tok_line.reshape(line * tok_rows, width)
     own_meta = lax.dynamic_index_in_dim(cot_line[:, :, :, share:], lax.axis_index(DP), 1, keepdims=False)
     own_meta = own_meta.reshape(line * tok_rows, META)
@@ -231,10 +230,10 @@
     block_cols = hidden_units // groups
     piece_rows = share // experts
     pieces = updated.reshape(experts, piece_rows, groups, block_cols).transpose(0, 2, 1, 3)
-    pieces = pieces.reshape(experts * groups, piece_rows * block_cols)
+    pieces = pieces.reshape(experts * groups, CAP, piece_rows * block_cols // CAP)
     spread = lax.all_to_all(pieces, EXPERT + DP, split_axis=0, concat_axis=0, tiled=True)
-    spread = spread.reshape(experts, groups * piece_rows * block_cols)
-    picked = jnp.take(spread, placement, axis=0)
+    spread = spread.reshape(experts, CAP, groups * piece_rows * block_cols // CAP)
+    picked = jnp.take(spread, placement, axis=0, mode="clip")
     landed = lax.all_to_all(picked, EXPERT, split_axis=0, concat_axis=0, tiled=True)
     landed = landed.reshape(experts, groups, piece_rows, block_cols).transpose(1, 0, 2, 3)
     return landed.reshape(1, width, block_cols)

time: 429 us -> 409 us (0.953)
  waiting for transfers between devices: 250 us -> 132 us
  Pallas kernels: 49.9 us -> 165 us
  other arithmetic: 14.1 us -> 1.99 us
  local copies, waits for them, and re-layouts: 17.2 us -> 12.9 us
    all_gather x1, waiting for transfers between devices: 133 us -> 0.02 us  [shards(): weights = lax.all_gather(gate_up[0], DP, axis=0, tiled=True)]
    pallas_call x1, Pallas kernels: 49.9 us -> 165 us  [line_gather(): pl.pallas_call(line_gather_kernel, out_shape=(jax.ShapeDtypeStruct((LINE,...]
    all_to_all x2 -> x0, other arithmetic: 10.2 us -> none  [shards(): lax.all_to_all(pieces, EXPERT + DP, split_axis=0, concat_axis=0, tiled=True)]
    all_to_all x1, waiting for transfers between devices: 0.01 us -> 10.2 us  [shards(): lax.all_to_all(rows.reshape(plane, line * CAP, width), PLANE, split_axis=...]
    unnamed x16 -> x18, local copies, waits for them, and re-layouts: 4.93 us -> 0.44 us
  transfers between devices with their start and end apart: 5 -> 5, of which waited for: 4 -> 4; matrix products, arithmetic and copies ran while one was open for 2% -> 2% of each run, Pallas kernels for 0% -> 40%
where the time goes in v4:
time: 409 us
  Pallas kernels  165 us (40%)
  waiting for transfers between devices  132 us (32%)
  blocking collectives  48.3 us (12%)
  starting transfers between devices  22.3 us (5%)
  between operations  13.7 us (3%)
  matrix products  13 us (3%)
  local copies, waits for them, and re-layouts  12.9 us (3%)
    pallas_call x1, Pallas kernels, line_gather(): pl.pallas_call(line_gather_kernel, out_shape=(jax.ShapeDtypeStruct((LINE,...  165 us
    all_gather x1, waiting for transfers between devices, shards(): hidden = lax.all_gather(hidden, DP, axis=0, tiled=True)  64.6 us
    all_to_all x1, blocking collectives, shards(): lax.all_to_all(picked, EXPERT, split_axis=0, concat_axis=0, tiled=True)  48.3 us
    all_to_all x1, waiting for transfers between devices, shards(): lax.all_to_all(pieces, EXPERT + DP, split_axis=0, concat_axis=0, tiled=True)  46.3 us
    all_to_all x1, starting transfers between devices, shards(): lax.all_to_all(pieces, EXPERT + DP, split_axis=0, concat_axis=0, tiled=True)  10.5 us
    all_to_all x1, waiting for transfers between devices, shards(): lax.all_to_all(rows.reshape(plane, line * CAP, width), PLANE, split_axis=...  10.2 us
    all_to_all x1, waiting for transfers between devices, shards(): lax.all_to_all(scaled.reshape(plane, line * groups * CAP, share), PLANE,...  10.1 us
  transfers between devices with their start and end apart: 5, of which 4 were waited for; matrix products, arithmetic and copies ran while one was open for 2% of the time, Pallas kernels for 40%

profile of v4, /device:TPU:1, one launch (start us, length us, event | category | flops | bytes accessed | tf_op | source)
XLA Modules:
  0.0 408.6 jit_solution(7329922632833036799)
XLA Ops:
  6.5 0.0 all-gather.6.cloned.1.call-start
  6.5 0.7 all-gather.6.cloned.1.call-update
  7.3 0.1 copy-done.2
  7.4 0.1 copy.48
  7.5 0.1 copy.49
  7.6 0.1 pad.4.clone
  7.6 0.1 maximum_maximum_fusion
  7.7 0.6 pad_maximum_fusion.cot_ref
  8.4 164.6 %shard_map.91 = (bf16[8,16,2048]{2,1,0:T(8,128)(2,1)}, bf16[8,4,16,640]{3,2,1,0:T(8,128)(2,1)}) custom-call(bf16[16,2048]{1,0:T(8,128)(2,1)} %tok_ref.1, bf16[4,16,640]{2,1,0:T(8,128)(2,1)} %pad_maximum_fusion.cot_ref), custom_call_target="tpu_custom_call" | custom-call | tf_op jit(solution)/shard_map/pallas_call | solution.py:129
  173.0 1.1 fusion.78
  174.1 0.1 copy.58
  174.2 0.1 copy.59
  174.3 0.1 fusion.29
  174.5 0.7 fusion.11
  175.2 2.0 convolution_convert_fusion.1
  177.2 7.5 %all-to-all-start = ((bf16[16,64,512]{2,1,0:T(8,128)(2,1)}), bf16[16,64,512]{2,1,0:T(8,128)(2,1)S(1)}, u32[]{:S(2)}, u32[]{:S(2)}) async-start(bf16[16,64,512]{2,1,0:T(8,128)(2,1)} %bitcast.5), calls=%async_computation | async-start | bytes 2097152 | tf_op jit(solution)/shard_map/all_to_all | solution.py:211
  184.8 0.1 copy.60
  184.9 0.1 convert_reduce_fusion
  185.0 0.2 fusion.12
  185.2 1.6 convolution_convert_fusion
  186.8 10.1 %all-to-all-done = bf16[16,64,512]{2,1,0:T(8,128)(2,1)S(1)} async-done(((bf16[16,64,512]{2,1,0:T(8,128)(2,1)}), bf16[16,64,512]{2,1,0:T(8,128)(2,1)S(1)}, u32[]{:S(2)}, u32[]{:S(2)}) %all-to-all-start) | async-done | bytes 1048608 | tf_op jit(solution)/shard_map/all_to_all | solution.py:211
  196.9 4.3 %all-to-all-start.1 = ((bf16[16,16,2048]{2,1,0:T(8,128)(2,1)}), bf16[16,16,2048]{2,1,0:T(8,128)(2,1)S(1)}, u32[]{:S(2)}, u32[]{:S(2)}) async-start(bf16[16,16,2048]{2,1,0:T(8,128)(2,1)} %bitcast.9), calls=%async_computation.1 | async-start | bytes 2097152 | tf_op jit(solution)/shard_map/all_to_all | solution.py:205
  201.3 0.0 all-gather.4.cloned.1.call-start
  201.3 0.4 reshape.226
  201.8 0.7 copy.52
  202.5 0.4 reshape.227
  202.9 0.0 all-gather.6.cloned.1.call-done
  203.0 10.2 %all-to-all-done.1 = bf16[16,16,2048]{2,1,0:T(8,128)(2,1)S(1)} async-done(((bf16[16,16,2048]{2,1,0:T(8,128)(2,1)}), bf16[16,16,2048]{2,1,0:T(8,128)(2,1)S(1)}, u32[]{:S(2)}, u32[]{:S(2)}) %all-to-all-start.1) | async-done | bytes 1048608 | tf_op jit(solution)/shard_map/all_to_all | solution.py:205
  213.1 4.6 %fusion.79 = f32[256,1536]{1,0:T(8,128)S(1)} fusion(bf16[256,2048]{1,0:T(8,128)(2,1)S(1)} %bitcast.45, bf16[2048,1536]{1,0:T(8,128)(2,1)} %bitcast.52), kind=kOutput, calls=%fused_computation.125 | convolution fusion | flops 1610612736 | bytes 8912896 | tf_op jit(solution)/shard_map/dot_general | solution.py:218
  217.7 0.0 copy-start.6
  217.7 1.0 fusion.22
  218.7 0.0 all-gather.4.cloned.1.call-update
  218.7 64.6 %all-gather.4.cloned.1.call-done = bf16[1024,768]{1,0:T(8,128)(2,1)} async-done(((bf16[256,768]{1,0:T(8,128)(2,1)}), bf16[1024,768]{1,0:T(8,128)(2,1)}) %all-gather.4.cloned.1.call-update) | async-done | bytes 1572880 | tf_op jit(solution)/shard_map/all_gather | solution.py:220
  283.3 3.9 fusion.8
  287.2 0.9 reshape.232
  288.1 0.4 copy.54
  288.5 0.0 copy-start.5
  288.5 2.1 reshape.233
  290.6 10.5 %all-to-all-start.2 = ((bf16[512,2,384]{2,1,0:T(2,128)(2,1)}), bf16[512,2,384]{2,1,0:T(2,128)(2,1)S(1)}, u32[]{:S(2)}, u32[]{:S(2)}) async-start(bf16[512,2,384]{2,1,0:T(2,128)(2,1)} %reshape.233), calls=%async_computation.2 | async-start | bytes 1572864 | tf_op jit(solution)/shard_map/all_to_all | solution.py:234
  301.1 0.0 copy-done.5
  301.1 46.3 %all-to-all-done.2 = bf16[512,2,384]{2,1,0:T(2,128)(2,1)S(1)} async-done(((bf16[512,2,384]{2,1,0:T(2,128)(2,1)}), bf16[512,2,384]{2,1,0:T(2,128)(2,1)S(1)}, u32[]{:S(2)}, u32[]{:S(2)}) %all-to-all-start.2) | async-done | bytes 786464 | tf_op jit(solution)/shard_map/all_to_all | solution.py:234
  347.4 0.5 reshape.234
  347.9 2.2 gather_fusion
  350.1 48.3 %all_to_all.20 = bf16[128,2,1536]{2,1,0:T(2,128)(2,1)S(1)} all-to-all(bf16[128,2,1536]{2,1,0:T(2,128)(2,1)S(1)} %gather_fusion), channel_id=1, replica_groups=mesh['x'=4,'zl'=8,'y'=4,'zh'=2,'core'=2] {'x','zl','y'}, dimensions={0} | all-to-all | bytes 1572864 | tf_op jit(solution)/shard_map/all_to_all | solution.py:237
  398.4 0.8 copy.55
  399.1 0.7 copy.56
  399.9 0.7 reshape.236
  400.5 1.2 copy.57
  (27 shorter events, 0.2 us)
Async XLA Ops:
  6.5 0.8 copy-start.2
  6.5 0.8 copy-start.3
  6.5 0.9 copy-start.4
  6.5 196.4 %all-gather.6.cloned.1.call-start = ((), (), s32[]{:S(2)}) async-start(), calls=%async_computation.5 | async-start | bytes 7864320 | tf_op jit(solution)/shard_map/all_gather | solution.py:201
  173.0 2.2 copy-start.1
  177.2 8.0 %copy-start = (bf16[8,16,2048]{2,1,0:T(8,128)(2,1)S(1)}, bf16[8,16,2048]{2,1,0:T(8,128)(2,1)}, u32[]{:S(2)}) copy-start(bf16[8,16,2048]{2,1,0:T(8,128)(2,1)} %get-tuple-element.11) | copy-start | bytes 1572868
  177.2 19.7 %all-to-all-start = ((bf16[16,64,512]{2,1,0:T(8,128)(2,1)}), bf16[16,64,512]{2,1,0:T(8,128)(2,1)S(1)}, u32[]{:S(2)}, u32[]{:S(2)}) async-start(bf16[16,64,512]{2,1,0:T(8,128)(2,1)} %bitcast.5), calls=%async_computation | async-start | bytes 2097152 | tf_op jit(solution)/shard_map/all_to_all | solution.py:211
  196.9 16.2 %all-to-all-start.1 = ((bf16[16,16,2048]{2,1,0:T(8,128)(2,1)}), bf16[16,16,2048]{2,1,0:T(8,128)(2,1)S(1)}, u32[]{:S(2)}, u32[]{:S(2)}) async-start(bf16[16,16,2048]{2,1,0:T(8,128)(2,1)} %bitcast.9), calls=%async_computation.1 | async-start | bytes 2097152 | tf_op jit(solution)/shard_map/all_to_all | solution.py:205
  201.3 82.0 %all-gather.4.cloned.1.call-start = ((), (), s32[]{:S(2)}) async-start(), calls=%async_computation.4 | async-start | bytes 1966080 | tf_op jit(solution)/shard_map/all_gather | solution.py:220
  217.7 65.6 %copy-start.6 = (bf16[1,512,768]{2,1,0:T(8,128)(2,1)S(1)}, bf16[1,512,768]{2,1,0:T(8,128)(2,1)}, u32[]{:S(2)}) copy-start(bf16[1,512,768]{2,1,0:T(8,128)(2,1)} %param.16) | copy-start | bytes 2359300
  288.5 12.6 %copy-start.5 = (s32[128]{0:T(128)S(1)}, s32[128]{0:T(128)}, u32[]{:S(2)}) copy-start(s32[128]{0:T(128)} %param.17) | copy-start | bytes 1540
  290.6 56.8 %all-to-all-start.2 = ((bf16[512,2,384]{2,1,0:T(2,128)(2,1)}), bf16[512,2,384]{2,1,0:T(2,128)(2,1)S(1)}, u32[]{:S(2)}, u32[]{:S(2)}) async-start(bf16[512,2,384]{2,1,0:T(2,128)(2,1)} %reshape.233), calls=%async_computation.2 | async-start | bytes 1572864 | tf_op jit(solution)/shard_map/all_to_all | solution.py:234
Sparse Core Ops, SparseCore 0:
  9.4 79.1 all-gather.5
  218.8 64.4 all-gather.3

commit v5 on v4

--- a/solution.py
+++ b/solution.py
@@ -206,6 +206,7 @@
         rows.reshape(plane, line * CAP, width), PLANE, split_axis=0, concat_axis=0, tiled=True
     ).reshape(plane * line * CAP, width)
 
+    rows, cot_pack = lax.optimization_barrier((rows, cot_pack))
     _, cot_pick = pickers(cot_pack[:, share:], line * groups, tok_rows, top)
     scaled = jnp.dot(cot_pick, cot_pack[:, :share], preferred_element_type=jnp.float32).astype(bf16)
     scaled = lax.all_to_all(
@@ -214,7 +215,6 @@
     scaled = scaled.reshape(plane * line, groups, CAP, share).transpose(1, 0, 2, 3)
     scaled = scaled.reshape(groups * plane * line * CAP, share)
 
-    weights, scaled = lax.optimization_barrier((weights, scaled))
     pre = jnp.dot(rows, weights, preferred_element_type=jnp.float32)
     hidden = (jax.nn.silu(pre[:, :hidden_units]) * pre[:, hidden_units:]).astype(bf16)
     hidden = lax.all_gather(hidden, DP, axis=0, tiled=True)

time: 409 us -> 388 us (0.949)
  waiting for transfers between devices: 132 us -> 87.9 us
  blocking collectives: 48.3 us -> 83.3 us
  starting transfers between devices: 22.3 us -> 10.5 us
    all_to_all x0 -> x2, blocking collectives: none -> 35 us  [the longest x1 18.9 us: shards(): lax.all_to_all(rows.reshape(plane, line * CAP, width), PLANE, split_axis=...]
    all_gather x1, waiting for transfers between devices: 64.6 us -> 40.9 us  [shards(): hidden = lax.all_gather(hidden, DP, axis=0, tiled=True)]
    all_to_all x2 -> x0, waiting for transfers between devices: 20.3 us -> none  [the longest x1 10.2 us: shards(): lax.all_to_all(rows.reshape(plane, line * CAP, width), PLANE, split_axis=...]
    all_to_all x2 -> x0, starting transfers between devices: 11.8 us -> none  [the longest x1 7.51 us: shards(): lax.all_to_all(scaled.reshape(plane, line * groups * CAP, share), PLANE,...]
  transfers between devices with their start and end apart: 5 -> 3, of which waited for: 4 -> 2; matrix products, arithmetic and copies ran while one was open for 2% -> 2% of each run, Pallas kernels for 40% -> 42%
where the time goes in v5:
time: 388 us
  Pallas kernels  165 us (43%)
  waiting for transfers between devices  87.9 us (23%)
  blocking collectives  83.3 us (21%)
  between operations  13.7 us (4%)
  matrix products  13.1 us (3%)
  local copies, waits for them, and re-layouts  12.6 us (3%)
  starting transfers between devices  10.5 us (3%)
    pallas_call x1, Pallas kernels, line_gather(): pl.pallas_call(line_gather_kernel, out_shape=(jax.ShapeDtypeStruct((LINE,...  165 us
    all_to_all x1, blocking collectives, shards(): lax.all_to_all(picked, EXPERT, split_axis=0, concat_axis=0, tiled=True)  48.3 us
    all_to_all x1, waiting for transfers between devices, shards(): lax.all_to_all(pieces, EXPERT + DP, split_axis=0, concat_axis=0, tiled=True)  46.3 us
    all_gather x1, waiting for transfers between devices, shards(): hidden = lax.all_gather(hidden, DP, axis=0, tiled=True)  40.9 us
    all_to_all x1, blocking collectives, shards(): lax.all_to_all(rows.reshape(plane, line * CAP, width), PLANE, split_axis=...  18.9 us
    all_to_all x1, blocking collectives, shards(): lax.all_to_all(scaled.reshape(plane, line * groups * CAP, share), PLANE,...  16.1 us
    all_to_all x1, starting transfers between devices, shards(): lax.all_to_all(pieces, EXPERT + DP, split_axis=0, concat_axis=0, tiled=True)  10.5 us
  transfers between devices with their start and end apart: 3, of which 2 were waited for; matrix products, arithmetic and copies ran while one was open for 2% of the time, Pallas kernels for 42%

profile of v5, /device:TPU:1, one launch (start us, length us, event | category | flops | bytes accessed | tf_op | source)
XLA Modules:
  0.0 387.6 jit_solution(1839474248102573136)
XLA Ops:
  6.5 0.0 all-gather.6.cloned.1.call-start
  6.5 0.7 all-gather.6.cloned.1.call-update
  7.3 0.0 all-gather.4.cloned.1.call-start
  7.3 0.0 copy-done.2
  7.3 0.1 copy.48
  7.4 0.0 copy-done.3
  7.4 0.1 copy.49
  7.5 0.0 copy-done.1
  7.5 0.1 pad.4.clone
  7.6 0.1 maximum_maximum_fusion
  7.7 0.6 pad_maximum_fusion.cot_ref
  8.3 164.5 %shard_map.91 = (bf16[8,16,2048]{2,1,0:T(8,128)(2,1)}, bf16[8,4,16,640]{3,2,1,0:T(8,128)(2,1)}) custom-call(bf16[16,2048]{1,0:T(8,128)(2,1)} %tok_ref.1, bf16[4,16,640]{2,1,0:T(8,128)(2,1)} %pad_maximum_fusion.cot_ref), custom_call_target="tpu_custom_call" | custom-call | tf_op jit(solution)/shard_map/pallas_call | solution.py:129
  172.9 0.9 slice.24
  173.8 0.1 copy.58
  174.0 0.1 convert_reduce_fusion
  174.0 0.2 fusion.14
  174.2 1.7 convolution_convert_fusion
  175.9 18.9 %all_to_all.20 = bf16[16,16,2048]{2,1,0:T(8,128)(2,1)S(1)} all-to-all(bf16[16,16,2048]{2,1,0:T(8,128)(2,1)S(1)} %bitcast.44), channel_id=1, replica_groups=mesh['x'=4,'zl'=8,'y'=4,'zh'=2,'core'=2] {'x','y'}, dimensions={0} | all-to-all | bytes 2097152 | tf_op jit(solution)/shard_map/all_to_all | solution.py:205
  194.8 4.6 %fusion = f32[256,1536]{1,0:T(8,128)S(1)} fusion(bf16[256,2048]{1,0:T(8,128)(2,1)S(1)} %bitcast.48, bf16[1,2048,1536]{2,1,0:T(8,128)(2,1)} %all-gather.6.cloned.1.call-done), kind=kOutput, calls=%fused_computation.1 | convolution fusion | flops 1610612736 | bytes 8912896 | tf_op jit(solution)/shard_map/dot_general | solution.py:218
  199.4 0.0 copy-start
  199.4 1.0 fusion.24
  200.4 0.0 all-gather.4.cloned.1.call-update
  200.4 0.0 copy-done
  200.5 0.2 copy.51
  200.8 0.1 fusion.31
  200.9 0.7 fusion.13
  201.6 2.1 convolution_convert_fusion.1
  203.7 16.1 %all_to_all.21 = bf16[16,64,512]{2,1,0:T(8,128)(2,1)S(1)} all-to-all(bf16[16,64,512]{2,1,0:T(8,128)(2,1)S(1)} %bitcast.47), channel_id=1, replica_groups=mesh['x'=4,'zl'=8,'y'=4,'zh'=2,'core'=2] {'x','y'}, dimensions={0} | all-to-all | bytes 2097152 | tf_op jit(solution)/shard_map/all_to_all | solution.py:212
  219.7 0.4 reshape.230
  220.2 0.7 copy.53
  220.9 0.0 copy-start.5
  220.9 0.4 reshape.231
  221.4 40.9 %all-gather.4.cloned.1.call-done = bf16[1024,768]{1,0:T(8,128)(2,1)} async-done(((bf16[256,768]{1,0:T(8,128)(2,1)}), bf16[1024,768]{1,0:T(8,128)(2,1)}) %all-gather.4.cloned.1.call-update) | async-done | bytes 1572880 | tf_op jit(solution)/shard_map/all_gather | solution.py:220
  262.3 0.0 copy-done.5
  262.3 3.9 %fusion.10 = bf16[512,768]{1,0:T(8,128)(2,1)S(1)} fusion(bf16[1,512,768]{2,1,0:T(8,128)(2,1)S(1)} %copy-done.5, bf16[1,512,768]{2,1,0:T(8,128)(2,1)} %param.15, bf16[1,512,768]{2,1,0:T(8,128)(2,1)} %param.14, bf16[1024,512]{1,0:T(8,128)(2,1)S(1)} %reshape.231, bf16[1024,768]{1,0:T(8,128)(2,1)} %all-gather.4.cloned.1.call-done), kind=kOutput, calls=%fused_computation.15 | convolution fusion | flops 811991040 | bytes 5767168 | tf_op jit(solution)/shard_map/dot_general | solution.py:221
  266.2 0.9 reshape.232
  267.1 0.4 copy.54
  267.5 0.0 copy-start.4
  267.5 2.1 reshape.233
  269.6 10.5 %all-to-all-start.2 = ((bf16[512,2,384]{2,1,0:T(2,128)(2,1)}), bf16[512,2,384]{2,1,0:T(2,128)(2,1)S(1)}, u32[]{:S(2)}, u32[]{:S(2)}) async-start(bf16[512,2,384]{2,1,0:T(2,128)(2,1)} %reshape.233), calls=%async_computation.2 | async-start | bytes 1572864 | tf_op jit(solution)/shard_map/all_to_all | solution.py:234
  280.1 46.3 %all-to-all-done.2 = bf16[512,2,384]{2,1,0:T(2,128)(2,1)S(1)} async-done(((bf16[512,2,384]{2,1,0:T(2,128)(2,1)}), bf16[512,2,384]{2,1,0:T(2,128)(2,1)S(1)}, u32[]{:S(2)}, u32[]{:S(2)}) %all-to-all-start.2) | async-done | bytes 786464 | tf_op jit(solution)/shard_map/all_to_all | solution.py:234
  326.4 0.5 reshape.234
  326.9 2.2 gather_fusion
  329.1 48.3 %all_to_all.22 = bf16[128,2,1536]{2,1,0:T(2,128)(2,1)S(1)} all-to-all(bf16[128,2,1536]{2,1,0:T(2,128)(2,1)S(1)} %gather_fusion), channel_id=1, replica_groups=mesh['x'=4,'zl'=8,'y'=4,'zh'=2,'core'=2] {'x','zl','y'}, dimensions={0} | all-to-all | bytes 1572864 | tf_op jit(solution)/shard_map/all_to_all | solution.py:237
  377.3 0.8 copy.55
  378.1 0.7 copy.56
  378.8 0.7 reshape.236
  379.5 1.2 copy.57
  (20 shorter events, 0.1 us)
Async XLA Ops:
  6.5 0.8 copy-start.2
  6.5 0.9 copy-start.3
  6.5 1.0 copy-start.1
  6.5 188.3 %all-gather.6.cloned.1.call-start = ((), (), s32[]{:S(2)}) async-start(), calls=%async_computation.5 | async-start | bytes 7864320 | tf_op jit(solution)/shard_map/all_gather | solution.py:201
  7.3 255.0 %all-gather.4.cloned.1.call-start = ((), (), s32[]{:S(2)}) async-start(), calls=%async_computation.4 | async-start | bytes 1966080 | tf_op jit(solution)/shard_map/all_gather | solution.py:220
  199.4 1.1 copy-start
  220.9 41.4 %copy-start.5 = (bf16[1,512,768]{2,1,0:T(8,128)(2,1)S(1)}, bf16[1,512,768]{2,1,0:T(8,128)(2,1)}, u32[]{:S(2)}) copy-start(bf16[1,512,768]{2,1,0:T(8,128)(2,1)} %param.16) | copy-start | bytes 2359300
  267.5 12.6 %copy-start.4 = (s32[128]{0:T(128)S(1)}, s32[128]{0:T(128)}, u32[]{:S(2)}) copy-start(s32[128]{0:T(128)} %param.17) | copy-start | bytes 1540
  269.6 56.8 %all-to-all-start.2 = ((bf16[512,2,384]{2,1,0:T(2,128)(2,1)}), bf16[512,2,384]{2,1,0:T(2,128)(2,1)S(1)}, u32[]{:S(2)}, u32[]{:S(2)}) async-start(bf16[512,2,384]{2,1,0:T(2,128)(2,1)} %reshape.233), calls=%async_computation.2 | async-start | bytes 1572864 | tf_op jit(solution)/shard_map/all_to_all | solution.py:234
Sparse Core Ops, SparseCore 0:
  9.4 79.0 all-gather.5
  200.5 61.6 all-gather.3

commit v6 on v5

--- a/solution.py
+++ b/solution.py
@@ -26,8 +26,8 @@
 MESH = pl.DeviceIdType.MESH
 
 
-def line_gather_kernel(
-    tok_ref, cot_ref, tok_all, cot_all, tok_recv, tok_send, cot_recv, cot_send, dp_recv, dp_send, own_sem
+def tok_kernel(
+    tok_ref, tok_all, tok_recv, tok_send, own_sem
 ):
     at, zh, core = lax.axis_index("zl"), lax.axis_index("zh"), lax.axis_index("core")
     me = zh * 2 + core
@@ -44,9 +44,7 @@
         def _():
             pl.semaphore_signal(barrier, inc=1, device_id=ids[far], device_id_type=MESH)
 
-    for pz, pc in partners:
-        pl.semaphore_signal(barrier, inc=1, device_id={"zh": pz, "core": pc}, device_id_type=MESH)
-    pl.semaphore_wait(barrier, 3 + has[0].astype(jnp.int32) + has[1].astype(jnp.int32))
+    pl.semaphore_wait(barrier, has[0].astype(jnp.int32) + has[1].astype(jnp.int32))
 
     def hop(out, recv, send, block, far, source=None):
         return pltpu.make_async_remote_copy(
@@ -88,8 +86,79 @@
                 def _():
                     hop(out, recv, send, block, far, source if s == 0 else None).wait_send()
 
-    own_tok = pltpu.make_async_copy(tok_ref, tok_all.at[at], own_sem.at[0])
-    own_cot = pltpu.make_async_copy(cot_ref.at[me], cot_all.at[at, me], own_sem.at[1])
+    own = pltpu.make_async_copy(tok_ref, tok_all.at[at], own_sem.at[0])
+    tok = (tok_all, tok_recv, tok_send)
+    own.start()
+    first(*tok, tok_ref)
+    for s in range(1, LINE):
+        step(*tok, s)
+    own.wait()
+    finish(*tok, tok_ref)
+
+
+def cot_kernel(
+    cot_ref, cot_all, cot_recv, cot_send, dp_recv, dp_send, own_sem
+):
+    at, zh, core = lax.axis_index("zl"), lax.axis_index("zh"), lax.axis_index("core")
+    me = zh * 2 + core
+    has = (at < LINE - 1, at > 0)
+    ids = ({"zl": jnp.minimum(at + 1, LINE - 1)}, {"zl": jnp.maximum(at - 1, 0)})
+    partners = []
+    for dz, dc in ((0, 1), (1, 0), (1, 1)):
+        partners.append(((zh + dz) % 2, (core + dc) % 2))
+
+    barrier = pltpu.get_barrier_semaphore()
+    for far in (0, 1):
+
+        @pl.when(has[far])
+        def _():
+            pl.semaphore_signal(barrier, inc=1, device_id=ids[far], device_id_type=MESH)
+
+    for pz, pc in partners:
+        pl.semaphore_signal(barrier, inc=1, device_id={"zh": pz, "core": pc}, device_id_type=MESH)
+    pl.semaphore_wait(barrier, 3 + has[0].astype(jnp.int32) + has[1].astype(jnp.int32))
+
+    def hop(out, recv, send, block, far, source=None):
+        return pltpu.make_async_remote_copy(
+            src_ref=out.at[block] if source is None else source,
+            dst_ref=out.at[block],
+            send_sem=send.at[far, block],
+            recv_sem=recv.at[block],
+            device_id=ids[far],
+            device_id_type=MESH,
+        )
+
+    def first(out, recv, send, source=None):
+        for far in (0, 1):
+
+            @pl.when(has[far])
+            def _():
+                hop(out, recv, send, at, far, source).start()
+
+    def step(out, recv, send, s):
+        for far in (0, 1):
+            block = at - s if far == 0 else at + s
+            there = block >= 0 if far == 0 else block < LINE
+
+            @pl.when(there)
+            def _():
+                hop(out, recv, send, block, far).wait_recv()
+
+            @pl.when(there & has[far])
+            def _():
+                hop(out, recv, send, block, far).start()
+
+    def finish(out, recv, send, source=None):
+        for s in range(LINE):
+            for far in (0, 1):
+                block = at - s if far == 0 else at + s
+                there = block >= 0 if far == 0 else block < LINE
+
+                @pl.when(there & has[far])
+                def _():
+                    hop(out, recv, send, block, far, source if s == 0 else None).wait_send()
+
+    own_cot = pltpu.make_async_copy(cot_ref.at[me], cot_all.at[at, me], own_sem.at[0])
     swaps = [
         pltpu.make_async_remote_copy(
             src_ref=cot_ref.at[pz * 2 + pc],
@@ -101,50 +170,29 @@
         )
         for k, (pz, pc) in enumerate(partners)
     ]
-    tok = (tok_all, tok_recv, tok_send)
     cot = (cot_all, cot_recv, cot_send)
     for swap in swaps:
         swap.start()
-    first(*tok, tok_ref)
-    own_tok.start()
     own_cot.start()
-    lead = 3
-    for s in range(1, lead):
-        step(*tok, s)
     for swap in swaps:
         swap.wait()
     own_cot.wait()
     first(*cot)
-    for s in range(lead, LINE + lead - 1):
-        if s < LINE:
-            step(*tok, s)
-        step(*cot, s - lead + 1)
-    own_tok.wait()
-    finish(*tok, tok_ref)
+    for s in range(1, LINE):
+        step(*cot, s)
     finish(*cot)
 
 
-def line_gather(tok, cot):
+def line_gather(kernel, number, value, extra):
     dma = pltpu.SemaphoreType.DMA
     return pl.pallas_call(
-        line_gather_kernel,
-        out_shape=(
-            jax.ShapeDtypeStruct((LINE,) + tok.shape, tok.dtype),
-            jax.ShapeDtypeStruct((LINE,) + cot.shape, cot.dtype),
-        ),
-        in_specs=[pl.BlockSpec(memory_space=pltpu.VMEM)] * 2,
-        out_specs=(pl.BlockSpec(memory_space=pltpu.VMEM),) * 2,
-        scratch_shapes=[
-            dma((LINE,)),
-            dma((2, LINE)),
-            dma((LINE,)),
-            dma((2, LINE)),
-            dma((3,)),
-            dma((3,)),
-            dma((2,)),
-        ],
-        compiler_params=pltpu.CompilerParams(collective_id=0, has_side_effects=True),
-    )(tok, cot)
+        kernel,
+        out_shape=jax.ShapeDtypeStruct((LINE,) + value.shape, value.dtype),
+        in_specs=[pl.BlockSpec(memory_space=pltpu.VMEM)],
+        out_specs=pl.BlockSpec(memory_space=pltpu.VMEM),
+        scratch_shapes=[dma((LINE,)), dma((2, LINE))] + [dma((n,)) for n in extra],
+        compiler_params=pltpu.CompilerParams(collective_id=number, has_side_effects=True),
+    )(value)
 
 
 def pickers(meta, blocks, block_rows, top):
@@ -193,20 +241,19 @@
     cot_parts = jnp.concatenate(
         [cot_parts, jnp.broadcast_to(meta[None], (groups, tok_rows, META))], axis=2
     )
-    tok_line, cot_line = line_gather(tokens, cot_parts)
-    tok_line = tok_line.reshape(line * tok_rows, width)
-    own_meta = lax.dynamic_index_in_dim(cot_line[:, :, :, share:], lax.axis_index(DP), 1, keepdims=False)
-    own_meta = own_meta.reshape(line * tok_rows, META)
-    cot_pack = cot_line.reshape(line * groups * tok_rows, share + META)
+    tok_pack = line_gather(tok_kernel, 0, jnp.concatenate([tokens, meta], axis=1), (1,))
+    tok_pack = tok_pack.reshape(line * tok_rows, width + META)
     weights = lax.all_gather(gate_up[0], DP, axis=0, tiled=True)
 
-    tok_pick, _ = pickers(own_meta, line, tok_rows, top)
-    rows = jnp.dot(tok_pick, tok_line, preferred_element_type=jnp.float32).astype(bf16)
+    tok_pick, _ = pickers(tok_pack[:, width:], line, tok_rows, top)
+    rows = jnp.dot(tok_pick, tok_pack[:, :width], preferred_element_type=jnp.float32).astype(bf16)
     rows = lax.all_to_all(
         rows.reshape(plane, line * CAP, width), PLANE, split_axis=0, concat_axis=0, tiled=True
     ).reshape(plane * line * CAP, width)
 
-    rows, cot_pack = lax.optimization_barrier((rows, cot_pack))
+    rows, cot_parts = lax.optimization_barrier((rows, cot_parts))
+    cot_line = line_gather(cot_kernel, 1, cot_parts, (3, 3, 1))
+    cot_pack = cot_line.reshape(line * groups * tok_rows, share + META)
     _, cot_pick = pickers(cot_pack[:, share:], line * groups, tok_rows, top)
     scaled = jnp.dot(cot_pick, cot_pack[:, :share], preferred_element_type=jnp.float32).astype(bf16)
     scaled = lax.all_to_all(

time: 388 us -> 413 us (1.064)
  waiting for transfers between devices: 87.9 us -> 117 us
  blocking collectives: 83.3 us -> 68.7 us
  starting transfers between devices: 10.5 us -> 19.3 us
    all_gather x1, waiting for transfers between devices: 0.01 us -> 58.3 us  [shards(): weights = lax.all_gather(gate_up[0], DP, axis=0, tiled=True)]
    all_gather x1, waiting for transfers between devices: 40.9 us -> 0.02 us  [shards(): hidden = lax.all_gather(hidden, DP, axis=0, tiled=True)]
    all_to_all x1 -> x0, blocking collectives: 18.9 us -> none  [shards(): lax.all_to_all(rows.reshape(plane, line * CAP, width), PLANE, split_axis=...]
    all_to_all x0 -> x1, waiting for transfers between devices: none -> 11.4 us  [shards(): lax.all_to_all(rows.reshape(plane, line * CAP, width), PLANE, split_axis=...]
    all_to_all x0 -> x1, starting transfers between devices: none -> 7.22 us  [shards(): lax.all_to_all(rows.reshape(plane, line * CAP, width), PLANE, split_axis=...]
    all_to_all x1, blocking collectives: 16.1 us -> 20.4 us  [shards(): lax.all_to_all(scaled.reshape(plane, line * groups * CAP, share), PLANE,...]
    pallas_call x1 -> x2, Pallas kernels: 165 us -> 164 us  [line_gather(): pl.pallas_call(kernel, out_shape=jax.ShapeDtypeStruct((LINE,) + value.sha...]
  transfers between devices with their start and end apart: 3 -> 4, of which waited for: 2 -> 3; matrix products, arithmetic and copies ran while one was open for 2% -> 3% of each run, Pallas kernels for 42% -> 40%
where the time goes in v6:
time: 413 us
  Pallas kernels  164 us (40%)
  waiting for transfers between devices  117 us (28%)
  blocking collectives  68.7 us (17%)
  starting transfers between devices  19.3 us (5%)
  local copies, waits for them, and re-layouts  14.8 us (4%)
  matrix products  14.1 us (3%)
  between operations  13.7 us (3%)
    pallas_call x2, Pallas kernels, line_gather(): pl.pallas_call(kernel, out_shape=jax.ShapeDtypeStruct((LINE,) + value.sha...  164 us
    all_gather x1, waiting for transfers between devices, shards(): weights = lax.all_gather(gate_up[0], DP, axis=0, tiled=True)  58.3 us
    all_to_all x1, blocking collectives, shards(): lax.all_to_all(picked, EXPERT, split_axis=0, concat_axis=0, tiled=True)  48.3 us
    all_to_all x1, waiting for transfers between devices, shards(): lax.all_to_all(pieces, EXPERT + DP, split_axis=0, concat_axis=0, tiled=True)  46.3 us
    all_to_all x1, blocking collectives, shards(): lax.all_to_all(scaled.reshape(plane, line * groups * CAP, share), PLANE,...  20.4 us
    all_to_all x1, starting transfers between devices, shards(): lax.all_to_all(pieces, EXPERT + DP, split_axis=0, concat_axis=0, tiled=True)  12.1 us
    all_to_all x1, waiting for transfers between devices, shards(): lax.all_to_all(rows.reshape(plane, line * CAP, width), PLANE, split_axis=...  11.4 us
  transfers between devices with their start and end apart: 4, of which 3 were waited for; matrix products, arithmetic and copies ran while one was open for 3% of the time, Pallas kernels for 40%

profile of v6, /device:TPU:1, one launch (start us, length us, event | category | flops | bytes accessed | tf_op | source)
XLA Modules:
  0.0 412.8 jit_solution(244608153322052913)
XLA Ops:
  6.5 0.7 all-gather.6.cloned.1.call-update
  7.3 0.1 copy.42
  7.4 0.1 copy.41
  7.4 0.7 concatenate.10.tok_ref
  8.2 29.1 %shard_map.91 = bf16[8,16,2176]{2,1,0:T(8,128)(2,1)} custom-call(bf16[16,2176]{1,0:T(8,128)(2,1)} %concatenate.10.tok_ref), custom_call_target="tpu_custom_call" | custom-call | tf_op jit(solution)/shard_map/pallas_call | solution.py:188
  37.3 0.8 slice.35
  38.0 0.1 copy.53
  38.2 0.1 convert_reduce_fusion
  38.3 0.2 fusion.14
  38.5 2.7 convolution_convert_fusion
  41.1 7.2 %all-to-all-start = ((bf16[16,16,2048]{2,1,0:T(8,128)(2,1)}), bf16[16,16,2048]{2,1,0:T(8,128)(2,1)S(1)}, u32[]{:S(2)}, u32[]{:S(2)}) async-start(bf16[16,16,2048]{2,1,0:T(8,128)(2,1)} %bitcast.3), calls=%async_computation | async-start | bytes 2097152 | tf_op jit(solution)/shard_map/all_to_all | solution.py:250
  48.4 0.0 all-gather.4.cloned.1.call-start
  48.4 0.1 pad_maximum_fusion.1
  48.5 0.6 pad_maximum_fusion.cot_ref
  49.2 11.4 %all-to-all-done = bf16[16,16,2048]{2,1,0:T(8,128)(2,1)S(1)} async-done(((bf16[16,16,2048]{2,1,0:T(8,128)(2,1)}), bf16[16,16,2048]{2,1,0:T(8,128)(2,1)S(1)}, u32[]{:S(2)}, u32[]{:S(2)}) %all-to-all-start) | async-done | bytes 1048608 | tf_op jit(solution)/shard_map/all_to_all | solution.py:250
  60.5 58.3 %all-gather.6.cloned.1.call-done = bf16[1,2048,1536]{2,1,0:T(8,128)(2,1)} async-done(((bf16[1,512,1536]{2,1,0:T(8,128)(2,1)}), bf16[1,2048,1536]{2,1,0:T(8,128)(2,1)}) %all-gather.6.cloned.1.call-update) | async-done | bytes 6291472 | tf_op jit(solution)/shard_map/all_gather | solution.py:246
  118.8 4.6 %fusion = f32[256,1536]{1,0:T(8,128)S(1)} fusion(bf16[256,2048]{1,0:T(8,128)(2,1)S(1)} %bitcast.47, bf16[1,2048,1536]{2,1,0:T(8,128)(2,1)} %all-gather.6.cloned.1.call-done), kind=kOutput, calls=%fused_computation.1 | convolution fusion | flops 1610612736 | bytes 8912896 | tf_op jit(solution)/shard_map/dot_general | solution.py:265
  123.4 1.0 fusion.24
  124.3 0.0 all-gather.4.cloned.1.call-update
  124.4 134.5 %shard_map.92 = bf16[8,4,16,640]{3,2,1,0:T(8,128)(2,1)} custom-call(bf16[4,16,640]{2,1,0:T(8,128)(2,1)} %pad_maximum_fusion.cot_ref), custom_call_target="tpu_custom_call" | custom-call | tf_op jit(solution)/shard_map/pallas_call | solution.py:188
  258.9 1.1 fusion.81
  260.1 0.1 copy.54
  260.2 0.1 copy.55
  260.3 0.1 fusion.32
  260.4 0.7 fusion.13
  261.1 0.0 copy-done
  261.1 2.1 convolution_convert_fusion.1
  263.2 20.4 %all_to_all.20 = bf16[16,64,512]{2,1,0:T(8,128)(2,1)S(1)} all-to-all(bf16[16,64,512]{2,1,0:T(8,128)(2,1)} %bitcast.48), channel_id=1, replica_groups=mesh['x'=4,'zl'=8,'y'=4,'zh'=2,'core'=2] {'x','y'}, dimensions={0} | all-to-all | bytes 2097152 | tf_op jit(solution)/shard_map/all_to_all | solution.py:259
  283.6 0.4 reshape.225
  284.0 0.7 copy.48
  284.7 0.0 copy-start.6
  284.7 0.4 reshape.226
  285.2 0.0 all-gather.4.cloned.1.call-done
  285.2 0.6 copy-done.6
  285.9 3.9 fusion.10
  289.7 0.9 reshape.227
  290.6 0.4 copy.49
  291.1 0.0 copy-start.5
  291.1 2.1 reshape.228
  293.2 12.1 %all-to-all-start.2 = ((bf16[512,2,384]{2,1,0:T(2,128)(2,1)}), bf16[512,2,384]{2,1,0:T(2,128)(2,1)S(1)}, u32[]{:S(2)}, u32[]{:S(2)}) async-start(bf16[512,2,384]{2,1,0:T(2,128)(2,1)} %reshape.228), calls=%async_computation.2 | async-start | bytes 1572864 | tf_op jit(solution)/shard_map/all_to_all | solution.py:281
  305.3 46.3 %all-to-all-done.2 = bf16[512,2,384]{2,1,0:T(2,128)(2,1)S(1)} async-done(((bf16[512,2,384]{2,1,0:T(2,128)(2,1)}), bf16[512,2,384]{2,1,0:T(2,128)(2,1)S(1)}, u32[]{:S(2)}, u32[]{:S(2)}) %all-to-all-start.2) | async-done | bytes 786464 | tf_op jit(solution)/shard_map/all_to_all | solution.py:281
  351.5 0.5 reshape.229
  352.0 2.2 gather_fusion
  354.2 48.3 %all_to_all.21 = bf16[128,2,1536]{2,1,0:T(2,128)(2,1)S(1)} all-to-all(bf16[128,2,1536]{2,1,0:T(2,128)(2,1)S(1)} %gather_fusion), channel_id=1, replica_groups=mesh['x'=4,'zl'=8,'y'=4,'zh'=2,'core'=2] {'x','zl','y'}, dimensions={0} | all-to-all | bytes 1572864 | tf_op jit(solution)/shard_map/all_to_all | solution.py:284
  402.5 0.8 copy.50
  403.3 0.7 copy.51
  404.0 0.7 reshape.231
  404.7 1.2 copy.52
  (26 shorter events, 0.1 us)
Async XLA Ops:
  6.5 0.7 copy-start.4
  6.5 0.8 copy-start.3
  6.5 0.9 copy-start.1
  6.5 112.3 %all-gather.6.cloned.1.call-start = ((), (), s32[]{:S(2)}) async-start(), calls=%async_computation.5 | async-start | bytes 7864320 | tf_op jit(solution)/shard_map/all_gather | solution.py:246
  38.5 10.0 %copy-start.2 = (bf16[16,2048]{1,0:T(8,128)(2,1)S(1)}, bf16[16,2048]{1,0:T(8,128)(2,1)}, u32[]{:S(2)}) copy-start(bf16[16,2048]{1,0:T(8,128)(2,1)} %param.10) | copy-start | bytes 196612
  41.1 19.4 %all-to-all-start = ((bf16[16,16,2048]{2,1,0:T(8,128)(2,1)}), bf16[16,16,2048]{2,1,0:T(8,128)(2,1)S(1)}, u32[]{:S(2)}, u32[]{:S(2)}) async-start(bf16[16,16,2048]{2,1,0:T(8,128)(2,1)} %bitcast.3), calls=%async_computation | async-start | bytes 2097152 | tf_op jit(solution)/shard_map/all_to_all | solution.py:250
  48.4 236.8 %all-gather.4.cloned.1.call-start = ((), (), s32[]{:S(2)}) async-start(), calls=%async_computation.4 | async-start | bytes 1966080 | tf_op jit(solution)/shard_map/all_gather | solution.py:267
  258.9 2.2 copy-start
  284.7 1.1 copy-start.6
  291.1 14.2 %copy-start.5 = (s32[128]{0:T(128)S(1)}, s32[128]{0:T(128)}, u32[]{:S(2)}) copy-start(s32[128]{0:T(128)} %param.17) | copy-start | bytes 1540
  293.2 58.4 %all-to-all-start.2 = ((bf16[512,2,384]{2,1,0:T(2,128)(2,1)}), bf16[512,2,384]{2,1,0:T(2,128)(2,1)S(1)}, u32[]{:S(2)}, u32[]{:S(2)}) async-start(bf16[512,2,384]{2,1,0:T(2,128)(2,1)} %reshape.228), calls=%async_computation.2 | async-start | bytes 1572864 | tf_op jit(solution)/shard_map/all_to_all | solution.py:281
Sparse Core Ops, SparseCore 0:
  9.4 109.3 all-gather.5
  124.5 109.3 all-gather.3
